TPU v7x, 256 devices: a whole 4x4x8 slice. The times are simulated.
256 devices in a mesh: gx: 32 (over z, x), gy: 8 (over y, core).
Axes of the slice: x: 4, y: 4, z: 8, core: 2. Of those that a mesh axis runs over, the one named last changes fastest.
Arguments:
- field: bfloat16 [20, 256, 128, 256], P(None, 'gx', 'gy'), may hold values from -6 to 6
- cotangent: bfloat16 [20, 256, 128, 256], P(None, 'gx', 'gy'), may hold values from -6 to 6
- spectral_weight: bfloat16 [2, 20, 20, 24, 2304], P(None, None, None, 'gy', 'gx'), may hold values from -6 to 6
- pointwise_weight: bfloat16 [20, 20], replicated, may hold values from -1.25 to 1.25
- bias: float32 [20], replicated, may hold values from -1 to 1
Outputs:
- output: bfloat16 [20, 256, 128, 256], P(None, 'gx', 'gy')
- grad_field: bfloat16 [20, 256, 128, 256], P(None, 'gx', 'gy')
- grad_spectral: float32 [2, 20, 20, 24, 2304], P(None, None, None, 'gy', 'gx')
- grad_pointwise: float32 [20, 20], replicated
- grad_bias: float32 [20], replicated
All inputs are finite; a program needn't handle non-finite values.
Results may differ from a plain program's by a relative error of at most 0.0013.
Values sent between devices are 32-bit elements; how exact they have to be, the bound alone decides.
A program may use at most 128 MiB of HBM per device.

v0:
```python
import math

import jax
import jax.numpy as jnp
from jax import lax
from jax.sharding import PartitionSpec as P

MX = 24
MY = 24
MZ = 24


PRECISE = lax.Precision.HIGHEST
TWO_PI = 2.0 * math.pi


def angles(frequencies, places, length):
    product = places[:, None] * frequencies[None, :] % length
    return product.astype(jnp.float32) * (TWO_PI / length)


def frequency(position, kept_modes, length):
    return jnp.where(position < kept_modes, position, position - 2 * kept_modes + length)


def forward_y(values, phases):
    cosine_table = jnp.cos(phases)
    sine_table = jnp.sin(phases)
    with_cos = jnp.einsum("brcxy,yj->brcxj", values, cosine_table, precision=PRECISE)
    with_sin = jnp.einsum("brcxy,yj->brcxj", values, sine_table, precision=PRECISE)
    real_part = with_cos[:, 0] + with_sin[:, 1]
    imag_part = with_cos[:, 1] - with_sin[:, 0]
    return jnp.stack([real_part, imag_part], axis=1)


def inverse_y(values, phases):
    cosine_table = jnp.cos(phases)
    sine_table = jnp.sin(phases)
    with_cos = jnp.einsum("brcxj,yj->brcxy", values, cosine_table, precision=PRECISE)
    with_sin = jnp.einsum("brcxj,yj->brcxy", values, sine_table, precision=PRECISE)
    real_part = with_cos[:, 0] - with_sin[:, 1]
    imag_part = with_sin[:, 0] + with_cos[:, 1]
    return jnp.stack([real_part, imag_part], axis=1)


def local(field, cotangent, spectral_weight, pointwise_weight, bias):
    channels, rows_x, rows_y, depth_cells = field.shape
    blocks_z = spectral_weight.shape[3]
    pair_rows = spectral_weight.shape[4]
    width_x = 2 * MX
    width_y = 2 * MY
    full_x = rows_x * lax.axis_size("gx")
    full_y = rows_y * lax.axis_size("gy")
    cell_count = float(full_x * full_y * depth_cells)
    place_x = lax.axis_index("gx")
    place_y = lax.axis_index("gy")
    own_x = place_x * rows_x + jnp.arange(rows_x, dtype=jnp.int32)
    freq_x = frequency(jnp.arange(width_x, dtype=jnp.int32), MX, full_x)
    freq_y = frequency(jnp.arange(width_y, dtype=jnp.int32), MY, full_y)
    phases_full_y = angles(freq_y, jnp.arange(full_y, dtype=jnp.int32), full_y)
    z_phases = angles(
        jnp.arange(MZ, dtype=jnp.int32), jnp.arange(depth_cells, dtype=jnp.int32), depth_cells
    )
    table_z = jnp.stack([jnp.cos(z_phases), -jnp.sin(z_phases)], axis=2).reshape(
        depth_cells, 2 * MZ
    )
    kz_own = place_y * blocks_z + jnp.arange(blocks_z, dtype=jnp.int32)
    weight_z = (jnp.where(kz_own == 0, 1.0, 2.0).astype(jnp.float32) / cell_count)[None, :, None]
    own_first = place_x * pair_rows
    flat_width = blocks_z * 2 * channels

    def kx_terms(values, places, first_pair, count):
        kx_count = min(count // width_y + 2, width_x)
        kx_first = jnp.minimum(first_pair // width_y, width_x - kx_count)
        kx_ids = kx_first + jnp.arange(kx_count, dtype=jnp.int32)
        phases = angles(frequency(kx_ids, MX, full_x), places, full_x)
        cosine_table = jnp.cos(phases)
        sine_table = jnp.sin(phases)
        real_part = jnp.einsum(
            "bcxj,xi->ijbc", values[:, 0], cosine_table, precision=PRECISE
        ) + jnp.einsum("bcxj,xi->ijbc", values[:, 1], sine_table, precision=PRECISE)
        imag_part = jnp.einsum(
            "bcxj,xi->ijbc", values[:, 1], cosine_table, precision=PRECISE
        ) - jnp.einsum("bcxj,xi->ijbc", values[:, 0], sine_table, precision=PRECISE)
        terms = jnp.stack([real_part, imag_part], axis=3).reshape(kx_count * width_y, flat_width)
        offset = first_pair - kx_first * width_y
        return lax.dynamic_slice_in_dim(terms, offset, count, 0)

    def analyze(values):
        flat = values.reshape(-1, depth_cells)
        spectra = jnp.einsum("zk,mz->km", table_z, flat, precision=PRECISE).reshape(
            2 * MZ, channels, rows_x, rows_y
        )
        columns = lax.all_to_all(spectra, "gy", split_axis=0, concat_axis=3, tiled=True)
        mode_data = forward_y(columns.reshape(blocks_z, 2, channels, rows_x, full_y), phases_full_y)
        portion = lax.all_gather(mode_data, "gx", axis=3, tiled=True)
        places = jnp.arange(portion.shape[3], dtype=jnp.int32)
        owned = kx_terms(portion, places, own_first, pair_rows)
        return jnp.transpose(owned.reshape(pair_rows, blocks_z, 2, channels), (2, 3, 1, 0))

    def synthesize(spectrum):
        portion = lax.all_gather(spectrum, "gx", axis=3, tiled=True)
        blocks = portion.reshape(2, channels, blocks_z, width_x, width_y)
        phases = angles(freq_x, own_x, full_x)
        cosine_table = jnp.cos(phases)
        sine_table = jnp.sin(phases)
        real_part = jnp.einsum(
            "cbij,xi->bcxj", blocks[0], cosine_table, precision=PRECISE
        ) - jnp.einsum("cbij,xi->bcxj", blocks[1], sine_table, precision=PRECISE)
        imag_part = jnp.einsum(
            "cbij,xi->bcxj", blocks[0], sine_table, precision=PRECISE
        ) + jnp.einsum("cbij,xi->bcxj", blocks[1], cosine_table, precision=PRECISE)
        mode_data = jnp.stack([real_part, imag_part], axis=1)
        fields = inverse_y(mode_data, phases_full_y)
        columns = lax.all_to_all(fields, "gy", split_axis=4, concat_axis=0, tiled=True)
        flat = columns.reshape(2 * MZ, -1)
        return jnp.einsum("km,zk->mz", flat, table_z, precision=PRECISE).reshape(
            channels, rows_x, rows_y, depth_cells
        )

    weights = spectral_weight.astype(jnp.float32)
    widened = field.astype(jnp.float32)
    spec_u = analyze(widened)
    mixed_re = jnp.einsum("cobp,cbp->obp", weights[0], spec_u[0], precision=PRECISE) - jnp.einsum(
        "cobp,cbp->obp", weights[1], spec_u[1], precision=PRECISE
    )
    mixed_im = jnp.einsum("cobp,cbp->obp", weights[0], spec_u[1], precision=PRECISE) + jnp.einsum(
        "cobp,cbp->obp", weights[1], spec_u[0], precision=PRECISE
    )
    mixed_modes = jnp.stack([mixed_re, mixed_im]) * weight_z
    conv = synthesize(mixed_modes)
    pointwise = jnp.dot(
        pointwise_weight.T, field.reshape(channels, -1), preferred_element_type=jnp.float32
    ).reshape(field.shape)
    preact = pointwise + bias[:, None, None, None] + conv
    activated, pullback = jax.vjp(jax.nn.gelu, preact)
    gradient = pullback(cotangent.astype(jnp.float32))[0]
    grad_mix = analyze(gradient) * weight_z
    spec_re = jnp.einsum("cobp,obp->cbp", weights[0], grad_mix[0], precision=PRECISE) + jnp.einsum(
        "cobp,obp->cbp", weights[1], grad_mix[1], precision=PRECISE
    )
    spec_im = jnp.einsum("cobp,obp->cbp", weights[0], grad_mix[1], precision=PRECISE) - jnp.einsum(
        "cobp,obp->cbp", weights[1], grad_mix[0], precision=PRECISE
    )
    grad_spec = jnp.stack([spec_re, spec_im])
    weight_re = jnp.einsum("cbp,obp->cobp", spec_u[0], grad_mix[0], precision=PRECISE) + jnp.einsum(
        "cbp,obp->cobp", spec_u[1], grad_mix[1], precision=PRECISE
    )
    weight_im = jnp.einsum("cbp,obp->cobp", spec_u[0], grad_mix[1], precision=PRECISE) - jnp.einsum(
        "cbp,obp->cobp", spec_u[1], grad_mix[0], precision=PRECISE
    )
    grad_spectral = jnp.stack([weight_re, weight_im])
    returned = synthesize(grad_spec)
    grad_flat = gradient.reshape(channels, -1)
    back_point = jnp.dot(
        pointwise_weight.astype(jnp.float32), grad_flat, precision=PRECISE
    ).reshape(field.shape)
    grad_field = (back_point + returned).astype(jnp.bfloat16)
    local_weight = jnp.dot(widened.reshape(channels, -1), grad_flat.T, precision=PRECISE)
    local_bias = jnp.sum(grad_flat, axis=1)
    summed_weight, summed_bias = lax.psum((local_weight, local_bias), ("gx", "gy"))
    shrink = cell_count ** (-0.5)
    return (
        activated.astype(jnp.bfloat16),
        grad_field,
        grad_spectral,
        summed_weight * shrink,
        summed_bias * shrink,
    )


def solution(mesh):
    placed = (
        P(None, "gx", "gy", None),
        P(None, "gx", "gy", None),
        P(None, None, None, "gy", "gx"),
        P(),
        P(),
    )
    return jax.shard_map(
        local,
        mesh=mesh,
        in_specs=placed,
        out_specs=(
            P(None, "gx", "gy", None),
            P(None, "gx", "gy", None),
            P(None, None, None, "gy", "gx"),
            P(),
            P(),
        ),
        check_vma=False,
    )
```

profile of v0, /device:TPU:1, one launch (start us, length us, event | category | flops | bytes accessed | tf_op | source)
XLA Modules:
  0.0 803.7 jit_solution(9280649417124723916)
XLA Ops:
  10.4 3.8 copy.294
  14.2 5.5 reshape.223
  19.7 6.6 all-to-all-start
  26.5 9.0 %all-to-all-done = f32[8,1,15360]{2,1,0:T(1,128)S(1)} async-done(((f32[8,1,15360]{2,1,0:T(1,128)}), f32[8,1,15360]{2,1,0:T(1,128)S(1)}, u32[]{:S(2)}, u32[]{:S(2)}) %all-to-all-start) | async-done | bytes 491552 | tf_op jit(solution)/shard_map/all_to_all | solution.py:94
  37.9 5.3 reshape.224
  43.3 6.3 copy.295
  49.6 3.1 reshape.183
  56.2 141.7 %all-gather.5.cloned.1.call-done = f32[3,2,20,256,48]{4,3,2,1,0:T(8,128)} async-done(((f32[3,2,20,8,48]{4,3,2,1,0:T(8,128)}), f32[3,2,20,256,48]{4,3,2,1,0:T(8,128)}) %all-gather.5.cloned.1.call-update) | async-done | bytes 5898256 | tf_op jit(solution)/shard_map/all_gather | solution.py:96
  197.9 7.2 fusion
  205.2 7.1 fusion.1
  212.2 4.3 fusion.35
  216.6 3.8 fusion.33
  222.3 91.0 %all-gather.7.cloned.1.call-done = f32[2,20,3,2304]{1,0,2,3:T(2,128)} async-done(((f32[2,20,3,72]{1,0,2,3:T(2,128)}), f32[2,20,3,2304]{1,0,2,3:T(2,128)}) %all-gather.7.cloned.1.call-update) | async-done | bytes 1105936 | tf_op jit(solution)/shard_map/all_gather | solution.py:102
  313.3 10.0 %fusion.244 = (f32[1,20,3,2304]{1,0,2,3:T(1,128)}, f32[1,20,3,2304]{1,0,2,3:T(1,128)}) fusion(f32[2,20,3,2304]{1,0,2,3:T(2,128)} %all-gather.7.cloned.1.call-done), kind=kLoop, calls=%fused_computation.296 | loop fusion | bytes 2211840 | tf_op jit(solution)/shard_map/slice | solution.py:109
  323.3 11.2 %copy.429 = f32[1,20,3,2304]{3,2,1,0:T(4,128)} copy(f32[1,20,3,2304]{1,0,2,3:T(1,128)} %get-tuple-element.59) | data formatting | bytes 1105920 | tf_op jit(solution)/shard_map/squeeze | solution.py:108
  339.8 11.2 %copy.430 = f32[1,20,3,2304]{3,2,1,0:T(4,128)} copy(f32[1,20,3,2304]{1,0,2,3:T(1,128)} %get-tuple-element.58) | data formatting | bytes 1105920 | tf_op jit(solution)/shard_map/squeeze | solution.py:109
  360.5 5.6 reshape.225
  366.0 5.4 all-to-all-start.1
  371.6 2.8 fusion.18
  374.4 6.1 all-to-all-done.1
  382.4 5.4 reshape.226
  387.8 5.8 copy.314
  393.6 4.4 reshape.186
  399.4 10.1 %fusion.241 = (f32[20]{0:T(128)}, f32[20,8,16,256]{3,0,2,1:T(8,128)S(1)}, bf16[20,8,16,256]{3,0,2,1:T(8,128)(2,1)}) fusion(bf16[20,8,16,256]{3,2,1,0:T(8,128)(2,1)} %param.6, f32[256,48,1,1]{0,1,2,3:T(8,128)S(1)} %reshape.194, f32[20,8,16,48]{3,2,1,0:T(8,128)} %bitcast.337, f32[20,8,16,256]{3,0,2,1:T(8,128)} %fusion.18, f32[20]{0:T(128)S(1)} %copy-done.25), kind=kOutput, calls=%fused_computation.294 | convolution fusion | flops 393871360 | bytes 8405152 | tf_op jit(solution)/shard_map/km,zk->mz/dot_general | solution.py:117
  413.8 3.8 copy.319
  417.5 5.3 reshape.227
  422.8 12.3 %all_to_all.60 = f32[8,1,15360]{2,1,0:T(1,128)S(1)} all-to-all(f32[8,1,15360]{2,1,0:T(1,128)S(1)} %reshape.227), channel_id=1, replica_groups=mesh['gx'=32,'gy'=8] {'gy'}, dimensions={0} | all-to-all | bytes 983040 | tf_op jit(solution)/shard_map/all_to_all | solution.py:94
  437.0 5.3 reshape.228
  442.3 6.3 copy.320
  448.6 3.1 reshape.189
  454.3 137.9 %all-gather.9.cloned.1.call-done = f32[3,2,20,256,48]{4,3,2,1,0:T(8,128)} async-done(((f32[3,2,20,8,48]{4,3,2,1,0:T(8,128)}), f32[3,2,20,256,48]{4,3,2,1,0:T(8,128)}) %all-gather.9.cloned.1.call-update) | async-done | bytes 5898256 | tf_op jit(solution)/shard_map/all_gather | solution.py:96
  592.2 7.2 fusion.4
  599.4 7.1 fusion.5
  606.5 3.9 fusion.31
  610.4 4.1 fusion.29
  620.8 3.5 copy.447
  627.0 78.9 %all-reduce = (f32[20,20]{0,1:T(8,128)S(1)}, f32[20]{0:T(128)S(1)}) all-reduce(f32[20,20]{0,1:T(8,128)S(1)} %fusion.36, f32[20]{0:T(128)S(1)} %copy-done.24), channel_id=1, replica_groups=mesh['gx'=32,'gy'=8] {'gx','gy'}, use_global_device_ids=true, to_apply=%region_0.1 | all-reduce | flops 420 | bytes 3360 | tf_op jit(solution)/shard_map/psum | solution.py:161
  706.0 5.0 fusion.246
  711.0 10.0 %fusion.243 = (f32[1,20,3,2304]{1,0,2,3:T(1,128)}, f32[1,20,3,2304]{1,0,2,3:T(1,128)}) fusion(f32[2,20,3,2304]{1,0,2,3:T(2,128)} %all-gather.11.cloned.1.call-done), kind=kLoop, calls=%fused_computation.295 | loop fusion | bytes 2211840 | tf_op jit(solution)/shard_map/slice | solution.py:109
  721.0 9.8 %copy.433 = f32[1,20,3,2304]{3,2,1,0:T(4,128)S(1)} copy(f32[1,20,3,2304]{1,0,2,3:T(1,128)} %get-tuple-element.57) | data formatting | bytes 1105920 | tf_op jit(solution)/shard_map/squeeze | solution.py:108
  735.0 9.8 %copy.434 = f32[1,20,3,2304]{3,2,1,0:T(4,128)S(1)} copy(f32[1,20,3,2304]{1,0,2,3:T(1,128)} %get-tuple-element.56) | data formatting | bytes 1105920 | tf_op jit(solution)/shard_map/squeeze | solution.py:109
  753.3 5.7 reshape.229
  759.0 4.4 all-to-all-start.3
  766.8 2.9 copy.448
  776.0 5.3 reshape.230
  781.4 5.8 copy.337
  787.2 4.4 reshape.192
  792.0 5.0 add_convert_fusion
  (146 shorter events, 69.4 us)
Async XLA Ops:
  7.2 1.3 copy-start
  8.5 401.0 %copy-start.10 = (f32[256,48,1,1]{0,1,2,3:T(8,128)}, f32[256,48,1,1]{0,1,2,3:T(8,128)S(1)}, u32[]{:S(2)}) copy-start(f32[256,48,1,1]{0,1,2,3:T(8,128)S(1)} %reshape.194) | copy-start | bytes 147460
  19.7 15.8 %all-to-all-start = ((f32[8,1,15360]{2,1,0:T(1,128)}), f32[8,1,15360]{2,1,0:T(1,128)S(1)}, u32[]{:S(2)}, u32[]{:S(2)}) async-start(f32[8,1,15360]{2,1,0:T(1,128)} %reshape.223), calls=%async_computation | async-start | bytes 983040 | tf_op jit(solution)/shard_map/all_to_all | solution.py:94
  26.4 171.6 %all-gather.5.cloned.1.call-start = ((), (), s32[]{:S(2)}) async-start(), calls=%async_computation.4 | async-start | bytes 16220160 | tf_op jit(solution)/shard_map/all_gather | solution.py:96
  52.7 2.7 copy-start.9
  55.0 258.3 %all-gather.7.cloned.1.call-start = ((), (), s32[]{:S(2)}) async-start(), calls=%async_computation.5 | async-start | bytes 7299072 | tf_op jit(solution)/shard_map/all_gather | solution.py:102
  55.3 161.3 %copy-start.18 = (s32[3]{0:T(128)}, s32[3]{0:T(128)S(1)}, u32[]{:S(2)}) copy-start(s32[3]{0:T(128)S(1)} %compare_select_fusion) | copy-start | bytes 40
  55.3 165.9 %copy-start.22 = (f32[3]{0:T(128)}, f32[3]{0:T(128)S(1)}, u32[]{:S(2)}) copy-start(f32[3]{0:T(128)S(1)} %fusion.144) | copy-start | bytes 40
  56.2 164.7 %copy-start.5 = (bf16[1,20,20,3,72]{4,0,3,2,1:T(2,128)(2,1)}, bf16[1,20,20,3,72]{4,0,3,2,1:T(2,128)(2,1)S(1)}, u32[]{:S(2)}) copy-start(bf16[1,20,20,3,72]{4,0,3,2,1:T(2,128)(2,1)S(1)} %get-tuple-element.70) | copy-start | bytes 518404
  197.9 14.3 %copy-start.1 = (f32[3,2,20,256,48]{4,3,2,1,0:T(8,128)S(1)}, f32[3,2,20,256,48]{4,3,2,1,0:T(8,128)}, u32[]{:S(2)}) copy-start(f32[3,2,20,256,48]{4,3,2,1,0:T(8,128)} %all-gather.5.cloned.1.call-done) | copy-start | bytes 17694724
  220.8 102.5 %copy-start.12 = (f32[3,72,20]{1,0,2:T(4,128)}, f32[3,72,20]{1,0,2:T(4,128)S(1)}, u32[]{:S(2)}) copy-start(f32[3,72,20]{1,0,2:T(4,128)S(1)} %copy.440) | copy-start | bytes 51844
  220.8 102.5 %copy-start.14 = (f32[3,72,20]{1,0,2:T(4,128)}, f32[3,72,20]{1,0,2:T(4,128)S(1)}, u32[]{:S(2)}) copy-start(f32[3,72,20]{1,0,2:T(4,128)S(1)} %copy.439) | copy-start | bytes 51844
  222.2 132.6 %copy-start.16 = (s32[8]{0:T(128)}, s32[8]{0:T(128)S(1)}, u32[]{:S(2)}) copy-start(s32[8]{0:T(128)S(1)} %iota_add_fusion.1) | copy-start | bytes 100
  360.5 11.1 %copy-start.20 = (bf16[20,20]{1,0:T(8,128)(2,1)S(1)}, bf16[20,20]{1,0:T(8,128)(2,1)}, u32[]{:S(2)}) copy-start(bf16[20,20]{1,0:T(8,128)(2,1)} %param.8) | copy-start | bytes 2404
  366.0 14.5 %all-to-all-start.1 = ((f32[8,1,15360]{2,1,0:T(1,128)}), f32[8,1,15360]{2,1,0:T(1,128)S(1)}, u32[]{:S(2)}, u32[]{:S(2)}) async-start(f32[8,1,15360]{2,1,0:T(1,128)} %reshape.225), calls=%async_computation.1 | async-start | bytes 983040 | tf_op jit(solution)/shard_map/all_to_all | solution.py:115
  371.4 220.8 %all-gather.9.cloned.1.call-start = ((), (), s32[]{:S(2)}) async-start(), calls=%async_computation.6 | async-start | bytes 16220160 | tf_op jit(solution)/shard_map/all_gather | solution.py:96
  393.6 5.8 copy-start.25
  409.5 1.6 copy-start.3
  451.7 140.5 %copy-start.19 = (s32[3]{0:T(128)S(1)}, s32[3]{0:T(128)}, u32[]{:S(2)}) copy-start(s32[3]{0:T(128)} %copy-done.18) | copy-start | bytes 40
  454.0 257.0 %all-gather.11.cloned.1.call-start = ((), (), s32[]{:S(2)}) async-start(), calls=%async_computation.7 | async-start | bytes 7299072 | tf_op jit(solution)/shard_map/all_gather | solution.py:102
  592.2 14.3 %copy-start.2 = (f32[3,2,20,256,48]{4,3,2,1,0:T(8,128)S(1)}, f32[3,2,20,256,48]{4,3,2,1,0:T(8,128)}, u32[]{:S(2)}) copy-start(f32[3,2,20,256,48]{4,3,2,1,0:T(8,128)} %all-gather.9.cloned.1.call-done) | copy-start | bytes 17694724
  610.3 4.5 copy-start.23
  610.3 4.6 copy-start.6
  610.3 4.6 copy-start.13
  610.4 4.6 copy-start.15
  620.8 3.6 copy-start.4
  624.4 2.7 copy-start.24
  624.4 81.6 %copy-start.21 = (bf16[20,20]{1,0:T(8,128)(2,1)S(1)}, bf16[20,20]{1,0:T(8,128)(2,1)}, u32[]{:S(2)}) copy-start(bf16[20,20]{1,0:T(8,128)(2,1)} %param.8) | copy-start | bytes 2404
  721.0 10.9 %copy-start.17 = (s32[8]{0:T(128)S(1)}, s32[8]{0:T(128)}, u32[]{:S(2)}) copy-start(s32[8]{0:T(128)} %copy-done.16) | copy-start | bytes 100
  759.0 15.2 %all-to-all-start.3 = ((f32[8,1,15360]{2,1,0:T(1,128)}), f32[8,1,15360]{2,1,0:T(1,128)S(1)}, u32[]{:S(2)}, u32[]{:S(2)}) async-start(f32[8,1,15360]{2,1,0:T(1,128)} %reshape.229), calls=%async_computation.3 | async-start | bytes 983040 | tf_op jit(solution)/shard_map/all_to_all | solution.py:115
  769.7 2.3 copy-start.7
  769.8 2.3 copy-start.8
  787.2 4.8 copy-start.11
Sparse Core Ops, SparseCore 0:
  55.1 142.7 all-gather.4
  222.3 90.9 all-gather.6
  454.2 137.9 all-gather.8
  617.8 91.3 all-gather.10
where the time goes:
time: 811 us; the launch traced here: 804 us
  waiting for transfers between devices  386 us (48%)
  local copies, waits for them, and re-layouts  188 us (23%)
  matrix products  93.9 us (12%)
  blocking collectives  91.2 us (11%)
  starting transfers between devices  17.2 us (2%)
  between operations  14.7 us (2%)
  other arithmetic  12.6 us (2%)
    all_gather x2, waiting for transfers between devices, analyze(): portion = lax.all_gather(mode_data, 'gx', axis=3, tiled=True)  280 us
    all_gather x2, waiting for transfers between devices, synthesize(): portion = lax.all_gather(spectrum, 'gx', axis=3, tiled=True)  91 us
    psum x1, blocking collectives, local(): lax.psum((local_weight, local_bias), ('gx', 'gy'))  78.9 us
    unnamed x71, local copies, waits for them, and re-layouts  60.5 us
    squeeze x4, local copies, waits for them, and re-layouts, synthesize(): blocks[0]  24.1 us
    squeeze x4, local copies, waits for them, and re-layouts, synthesize(): blocks[1]  24.1 us
    slice x2, local copies, waits for them, and re-layouts, synthesize(): blocks[1]  20.1 us
  transfers between devices with their start and end apart: 7, of which 5 were waited for; matrix products, arithmetic and copies ran while one was open for 4% of the time, Pallas kernels for 0%

commit v1 on v0

v1 whole, which is shorter than its diff:
```python
import functools

import jax
import jax.numpy as jnp
import numpy as np
from jax import lax
from jax.experimental import pallas as pl
from jax.experimental.pallas import tpu as pltpu
from jax.sharding import PartitionSpec as P

C = 20
NX, NY, NZ = 256, 128, 256
KX, KY, KZ = 48, 48, 24
GX, GY = 32, 8
CELLS = float(NX * NY * NZ)
F32 = jnp.float32
BF16 = jnp.bfloat16
MESH = pl.DeviceIdType.MESH
NN = (((1,), (0,)), ((), ()))
NT = (((1,), (1,)), ((), ()))
GELU_A = float(np.sqrt(2.0 / np.pi))
GELU_B = 0.044715


def halves(table):
    high = table.astype(BF16)
    low = (table - np.asarray(high, np.float64)).astype(BF16)
    return np.asarray(high), np.asarray(low)


def tables():
    kz, r, d = np.meshgrid(np.arange(3), np.arange(2), np.arange(8), indexing="ij")
    depth = (d * 3 + kz).reshape(-1, 1) * np.arange(NZ)[None, :] % NZ * (2 * np.pi / NZ)
    tz = np.where(r.reshape(-1, 1) == 0, np.cos(depth), -np.sin(depth))
    tz = np.concatenate(halves(tz), axis=0)

    fx = np.where(np.arange(KX) < 24, np.arange(KX), np.arange(KX) - 48 + NX)
    fy = np.where(np.arange(KY) < 24, np.arange(KY), np.arange(KY) - 48 + NY)
    phase = np.arange(NY)[:, None] * fy[None, :] % NY * (2 * np.pi / NY)
    cos, sin = np.cos(phase).reshape(8, 16, KY), np.sin(phase).reshape(8, 16, KY)
    y = np.zeros((8, 2, 16, 128))
    y[:, 0, :, 0:48], y[:, 0, :, 48:96] = cos, -sin
    y[:, 1, :, 0:48], y[:, 1, :, 48:96] = sin, cos
    yh, yl = halves(y.reshape(256, 128))

    g = np.arange(GX)
    first = 3 * (g // 2) + g % 2
    kx = first[:, None] + np.arange(2)[None, :]
    phase = fx[kx][:, :, None] * np.arange(NX)[None, None, :] % NX * (2 * np.pi / NX)
    both = np.stack([np.cos(phase), np.sin(phase)])
    both = both.reshape(2, GX, 2, GX, 8)
    eye = np.eye(2)
    ax = np.einsum("egtsx,mn->egmtsnx", both, eye).reshape(256, 512)
    bx = np.einsum("egtsx,mn->esmxgnt", both, eye).reshape(1024, 128)
    axh, axl = halves(ax)
    bxh, bxl = halves(bx)

    m = np.arange(64)
    kz_m = np.where(m < 48, m // 16, (m - 48) // 4)
    c_m = np.where(m < 48, m % 16, 16 + (m - 48) % 4)
    row = np.arange(120)
    sel_o = (row[None, :] // 6 == c_m[:, None]) & (row[None, :] % 6 // 2 == kz_m[:, None])
    row = np.arange(480)
    sel_c = (row[None, :] // 24 == c_m[:, None]) & (row[None, :] % 6 // 2 == kz_m[:, None])
    live = (m < 60)[:, None]
    sel_o = np.asarray((sel_o & live).astype(BF16))
    sel_c = np.asarray((sel_c & live).astype(BF16))
    return tz, yh, yl, axh, axl, bxh, bxl, sel_o, sel_c


def iota(shape, axis):
    return lax.broadcasted_iota(jnp.int32, shape, axis)


def dot(a, b, dims):
    return lax.dot_general(a, b, dims, preferred_element_type=F32)


def split(x):
    high = x.astype(BF16)
    return high, (x - high.astype(F32)).astype(BF16)


def dot3(a, b, dims):
    return dot(a[0], b[0], dims) + dot(a[0], b[1], dims) + dot(a[1], b[0], dims)


def pick(sel, x):
    high, low = split(x)
    return dot(sel, high, NN) + dot(sel, low, NN)


def kernel(
    field, cot, w, pw, bias, tz, yh, yl, axh, axl, bxh, bxl, sel_o, sel_c,
    out, gf, gs, small,
    fs, cs, gh, gl, pw1, pw2, bb, pws, sy, ry, sx, rx, sp, rp, wf, tmp,
    u1, u2, d1, d2, q1, q2, lw, ls, lr, ms, mr,
    sy_sem, ry_sem, sx_sem, rx_sem, sp_sem, rp_sem, l_sem,
):
    g = lax.axis_index("gx")
    yy = lax.axis_index("gy")
    even = lax.rem(g, 2) == 0

    barrier = pltpu.get_barrier_semaphore()

    def greet_y(k, _):
        pl.semaphore_signal(
            barrier, inc=1, device_id=(g, lax.rem(yy + k, GY)), device_id_type=MESH
        )
        return 0

    def greet_x(k, _):
        pl.semaphore_signal(
            barrier, inc=1, device_id=(lax.rem(g + k, GX), yy), device_id_type=MESH
        )
        return 0

    lax.fori_loop(1, GY, greet_y, 0)
    lax.fori_loop(1, GX, greet_x, 0)

    def send_y(st):
        for k in range(1, GY):
            d = lax.rem(yy + k, GY)
            pltpu.make_async_remote_copy(
                src_ref=sy.at[st, :, pl.ds(d * 32, 32), :],
                dst_ref=ry.at[st, :, pl.ds(yy * 32, 32), :],
                send_sem=sy_sem.at[st],
                recv_sem=ry_sem.at[st],
                device_id=(g, d),
                device_id_type=MESH,
            ).start()
        own = pl.ds(yy * 32, 32)
        pltpu.make_async_copy(
            sy.at[st, :, own, :], ry.at[st, :, own, :], ry_sem.at[st]
        ).start()

    def send_gx(src, dst, ssem, rsem, size):
        def body(k, _):
            d = lax.rem(g + k, GX)
            pltpu.make_async_remote_copy(
                src_ref=src.at[pl.ds(d * size, size)],
                dst_ref=dst.at[pl.ds(g * size, size)],
                send_sem=ssem,
                recv_sem=rsem,
                device_id=(d, yy),
                device_id_type=MESH,
            ).start()
            return 0

        lax.fori_loop(1, GX, body, 0)
        own = pl.ds(g * size, size)
        pltpu.make_async_copy(src.at[own], dst.at[own], rsem).start()

    def send_x(st):
        send_gx(sx.at[st], rx.at[st], sx_sem.at[st], rx_sem.at[st], 16)

    def send_p(st):
        send_gx(sp.at[st], rp.at[st], sp_sem.at[st], rp_sem.at[st], 1)

    def landed(ref, sem):
        pltpu.make_async_copy(ref, ref, sem).wait()

    lane = iota((64, 128), 1)

    def widen(c, _):
        rows = pl.ds(c * 128, 128)
        v = field[c].astype(F32).reshape(128, 256)
        fs[0, rows, :] = v[:, :128]
        fs[1, rows, :] = v[:, 128:]
        return 0

    lax.fori_loop(0, C, widen, 0)

    def rows_of(ref, y):
        rows = pl.ds(y, 160, stride=16)
        return jnp.concatenate([ref[0, rows, :], ref[1, rows, :]], axis=1)

    pad_rows = jnp.zeros((96, 256), BF16)

    def analyze_z(st, y, s):
        for r in range(2):
            rows = pl.ds(r * 16 + y, 8, stride=32)
            tail = None
            for kz in range(3):
                at = (kz * 2 + r) * 8
                sy[st, kz, rows, :] = s[at : at + 8, :128]
                piece = s[at : at + 8, 128:]
                tail = piece if kz == 0 else tail + pltpu.roll(piece, 32 * kz, 1)
            sy[st, 3, rows, :] = tail

    def synthesize_z(st, y):
        main, tail = [], []
        for kz in range(3):
            for r in range(2):
                rows = pl.ds(r * 16 + y, 8, stride=32)
                main.append(ry[st, kz, rows, :])
                piece = ry[st, 3, rows, :]
                tail.append(piece if kz == 0 else pltpu.roll(piece, 128 - 32 * kz, 1))
        data = jnp.concatenate(
            [jnp.concatenate(main, axis=0), jnp.concatenate(tail, axis=0)], axis=1
        )
        data = split(jnp.transpose(data)[:160])
        return dot3(data, (tz[0:48, :], tz[48:96, :]), NN)

    def first_y(y, _):
        f = jnp.concatenate([rows_of(fs, y).astype(BF16), pad_rows], axis=0)
        s = dot(tz[...], f, NT)
        analyze_z(0, y, s[0:48] + s[48:96])
        return 0

    lax.fori_loop(0, 16, first_y, 0)

    pl.semaphore_wait(barrier, GY - 1 + GX - 1)
    send_y(0)

    def widen_more(c, _):
        rows = pl.ds(c * 128, 128)
        v = cot[c].astype(F32).reshape(128, 256)
        cs[0, rows, :] = v[:, :128]
        cs[1, rows, :] = v[:, 128:]
        wf[c, :, 0:72] = w[c].astype(F32).reshape(120, 72)
        return 0

    wf[...] = jnp.zeros_like(wf)
    lax.fori_loop(0, C, widen_more, 0)

    pws[...] = jnp.zeros_like(pws)
    pws[0:20, 0:20] = pw[...].astype(F32)
    pws[32:33, 0:20] = bias[...]
    ones_e = iota((160, 128), 0) // 8 == iota((160, 128), 1)
    ones_e = jnp.where(ones_e, 1.0, 0.0)
    e = ones_e[:, :32].astype(BF16)
    same_x = lax.rem(iota((160, 160), 0), 8) == lax.rem(iota((160, 160), 1), 8)
    m = pws[0:32, 0:32].astype(BF16)
    t = dot(e, m, NT).astype(BF16)
    pw1[...] = jnp.where(same_x, dot(t, e, NT), 0.0).astype(BF16)
    t = dot(e, m, NN).astype(BF16)
    pw2[...] = jnp.where(same_x, dot(t, e, NT), 0.0).astype(BF16)
    column = jnp.sum(ones_e * pws[32:33, :], axis=1, keepdims=True)
    bb[...] = jnp.broadcast_to(column, (160, 128))

    def forward_y(st):
        for t in range(4):
            data = split(jnp.transpose(ry[st, t]))
            sx[st, pl.ds(t * 128, 128), :] = dot3(data, (yh[...], yl[...]), NN)

    def forward_x(st):
        p = dot3((axh[...], axl[...]), split(rx[st]), NN)
        pc, ps = p[:128], p[128:]
        side = iota((128, 128), 1) < 48
        o = pc + jnp.where(side, pltpu.roll(ps, 80, 1), -pltpu.roll(ps, 48, 1))
        sp[st] = o.reshape(32, 4, 128)

    def spectrum(st):
        tmp[...] = rp[st].reshape(128, 128)
        k0 = tmp[pl.ds(0, 64, stride=2), :]
        k1 = tmp[pl.ds(1, 64, stride=2), :]
        roll = lambda v, n: pltpu.roll(v, n, 1)
        re_e = jnp.where(lane < 48, k0, roll(k1, 48))
        im_e = jnp.where(lane < 48, roll(k0, 80), k1)
        re_o = jnp.where(lane < 24, roll(k0, 104), roll(k1, 24))
        im_o = jnp.where(lane < 24, roll(k0, 56), roll(k1, 104))
        live = lane < 72
        re = jnp.where(live, jnp.where(even, re_e, re_o), 0.0)
        im = jnp.where(live, jnp.where(even, im_e, im_o), 0.0)
        return re, im

    def modes(re, im, st):
        roll = lambda v, n: pltpu.roll(v, n, 1)
        within = lambda a, b: (lane >= a) & (lane < b)
        zero = jnp.zeros((64, 128), F32)
        e0 = jnp.where(lane < 48, re, jnp.where(within(48, 96), roll(im, 48), zero))
        e1 = jnp.where(lane < 24, roll(re, 80), jnp.where(within(48, 72), im, zero))
        o0 = jnp.where(
            within(24, 48), roll(re, 24), jnp.where(within(72, 96), roll(im, 72), zero)
        )
        o1 = jnp.where(lane < 48, roll(re, 104), jnp.where(within(48, 96), roll(im, 24), zero))
        tmp[pl.ds(0, 64, stride=2), :] = jnp.where(even, e0, o0)
        tmp[pl.ds(1, 64, stride=2), :] = jnp.where(even, e1, o1)
        sp[st] = tmp[...].reshape(32, 4, 128)

    def inverse_x(st):
        p = dot3((bxh[...], bxl[...]), split(rp[st].reshape(128, 128)), NN)
        pc, ps = p[:512], p[512:]
        side = iota((512, 128), 1) < 48
        sx[st] = pc + jnp.where(side, -pltpu.roll(ps, 80, 1), pltpu.roll(ps, 48, 1))

    def inverse_y(st):
        for t in range(4):
            data = split(rx[st, pl.ds(t * 128, 128), :])
            sy[st, t] = dot3((yh[...], yl[...]), data, NT)

    row64 = iota((64, 128), 0)
    zeroth = (row64 < 16) | ((row64 >= 48) & (row64 < 52))
    weight_z = jnp.where(zeroth & (yy == 0), 1.0 / CELLS, 2.0 / CELLS)

    landed(ry.at[0], ry_sem.at[0])
    forward_y(0)
    send_x(0)
    landed(rx.at[0], rx_sem.at[0])
    forward_x(0)
    send_p(0)
    landed(rp.at[0], rp_sem.at[0])
    re, im = spectrum(0)
    for kz in range(3):
        for o in range(4):
            for r in range(2):
                at = o * 6 + kz * 2 + r
                sign = 1.0 if r == 0 else -1.0
                most = pl.ds(at, 16, stride=24)
                rest = pl.ds(16 * 24 + at, 4, stride=24)
                u1[most, :] = re[kz * 16 : kz * 16 + 16]
                u1[rest, :] = re[48 + kz * 4 : 52 + kz * 4]
                u2[most, :] = sign * im[kz * 16 : kz * 16 + 16]
                u2[rest, :] = sign * im[48 + kz * 4 : 52 + kz * 4]

    real_row = lax.rem(iota((24, 128), 0), 2) == 0

    def mix(c, acc):
        a, b = acc
        rows = pl.ds(c * 24, 24)
        s1, s2 = u1[rows, :], u2[rows, :]
        sa = jnp.concatenate([jnp.where(real_row, s1, s2)] * 5, axis=0)
        sb = jnp.concatenate([jnp.where(real_row, s2, s1)] * 5, axis=0)
        return a + wf[c] * sa, b + wf[c] * sb

    zero = jnp.zeros((120, 128), F32)
    a, b = lax.fori_loop(0, C, mix, (zero, zero))
    modes(pick(sel_o[...], a) * weight_z, pick(sel_o[...], b) * weight_z, 1)
    send_p(1)
    landed(rp.at[1], rp_sem.at[1])
    inverse_x(1)
    send_x(1)
    landed(rx.at[1], rx_sem.at[1])
    inverse_y(1)
    send_y(1)
    landed(ry.at[1], ry_sem.at[1])

    lw[...] = jnp.zeros_like(lw)
    ones_rows = jnp.ones((16, 256), BF16)

    def middle(y, _):
        conv = synthesize_z(1, y)
        f = rows_of(fs, y).astype(BF16)
        v = dot(pw1[...], f, NN) + jnp.concatenate([bb[...], bb[...]], axis=1) + conv
        square = v * v
        t = jnp.tanh(GELU_A * v * (1.0 + GELU_B * square))
        half = 0.5 * (1.0 + t)
        act = v * half
        slope = half + (0.5 * GELU_A) * v * (1.0 - t * t) * (1.0 + (3.0 * GELU_B) * square)
        grad = rows_of(cs, y) * slope
        rows = pl.ds(y, 160, stride=16)
        fs[0, rows, :] = act[:, :128]
        fs[1, rows, :] = act[:, 128:]
        high, low = split(grad)
        gh[y] = high
        gl[y] = low
        f = jnp.concatenate([f, ones_rows], axis=0)
        lw[...] += dot(f, high, NT) + dot(f, low, NT)
        s = dot(tz[...], jnp.concatenate([high, pad_rows], axis=0), NT)
        s = s[0:48] + s[48:96]
        s = s + dot(tz[0:48, :], jnp.concatenate([low, pad_rows], axis=0), NT)
        analyze_z(2, y, s)
        return 0

    lax.fori_loop(0, 16, middle, 0)
    send_y(2)

    row, col = iota((176, 160), 0), iota((176, 160), 1)
    keep = (row >= 160) | (lax.rem(row, 8) == lax.rem(col, 8))
    total = jnp.where(keep, lw[...], 0.0)
    row, col = iota((32, 176), 0), iota((32, 176), 1)
    left = ((col < 160) & (col // 8 == row)) | ((row == 20) & (col == 160))
    left = jnp.where(left, 1.0, 0.0).astype(BF16)
    high, low = split(pick(left, total))
    e128 = ones_e.astype(BF16)
    ls[...] = dot(high, e128, NN) + dot(low, e128, NN)
    for k in range(1, GY):
        d = lax.rem(yy + k, GY)
        pltpu.make_async_remote_copy(
            src_ref=ls,
            dst_ref=lr.at[yy],
            send_sem=l_sem.at[0],
            recv_sem=l_sem.at[1],
            device_id=(g, d),
            device_id_type=MESH,
        ).start()
    pltpu.make_async_copy(ls, lr.at[yy], l_sem.at[1]).start()

    def write_out(c, _):
        rows = pl.ds(c * 128, 128)
        v = jnp.concatenate([fs[0, rows, :], fs[1, rows, :]], axis=1)
        out[c] = v.astype(BF16).reshape(8, 16, 256)
        return 0

    lax.fori_loop(0, C, write_out, 0)

    landed(ry.at[2], ry_sem.at[2])
    forward_y(2)
    send_x(2)

    landed(lr, l_sem.at[1])
    ms[...] = jnp.sum(lr[...], axis=0)

    def share(k, _):
        d = lax.rem(g + k, GX)
        pltpu.make_async_remote_copy(
            src_ref=ms,
            dst_ref=mr.at[g],
            send_sem=l_sem.at[2],
            recv_sem=l_sem.at[3],
            device_id=(d, yy),
            device_id_type=MESH,
        ).start()
        return 0

    lax.fori_loop(1, GX, share, 0)
    pltpu.make_async_copy(ms, mr.at[g], l_sem.at[3]).start()

    landed(rx.at[2], rx_sem.at[2])
    forward_x(2)
    send_p(2)
    landed(rp.at[2], rp_sem.at[2])
    re, im = spectrum(2)
    re, im = re * weight_z, im * weight_z
    for kz in range(3):
        for r in range(2):
            most = pl.ds(kz * 2 + r, 16, stride=6)
            rest = pl.ds(96 + kz * 2 + r, 4, stride=6)
            one, two = (re, im) if r == 0 else (im, re)
            d1[most, :] = one[kz * 16 : kz * 16 + 16]
            d1[rest, :] = one[48 + kz * 4 : 52 + kz * 4]
            d2[most, :] = two[kz * 16 : kz * 16 + 16]
            d2[rest, :] = two[48 + kz * 4 : 52 + kz * 4]

    even_row = lax.rem(iota((120, 128), 0), 2) == 0

    def unmix(c, _):
        rows = pl.ds(c * 24, 24)
        x1 = d1[...]
        x2 = jnp.where(even_row, d2[...], -d2[...])
        wc = wf[c]
        q1[rows, :] = jnp.sum((wc * x1).reshape(5, 24, 128), axis=0)
        q2[rows, :] = jnp.sum((wc * x2).reshape(5, 24, 128), axis=0)
        return 0

    lax.fori_loop(0, C, unmix, 0)
    modes(pick(sel_c[...], q1[...]), pick(sel_c[...], q2[...]), 3)
    send_p(3)

    def outer(c, _):
        rows = pl.ds(c * 24, 24)
        s1 = jnp.concatenate([u1[rows, :]] * 5, axis=0)
        s2 = jnp.concatenate([u2[rows, :]] * 5, axis=0)
        v = s1 * d1[...] + s2 * d2[...]
        gs[c] = v[:, 0:72].reshape(20, 3, 2, 72)
        return 0

    lax.fori_loop(0, C, outer, 0)

    landed(rp.at[3], rp_sem.at[3])
    inverse_x(3)
    send_x(3)
    landed(mr, l_sem.at[3])
    small[...] = jnp.sum(mr[...], axis=0) * (CELLS**-0.5)
    landed(rx.at[3], rx_sem.at[3])
    inverse_y(3)
    send_y(3)
    landed(ry.at[3], ry_sem.at[3])

    def last(y, _):
        back = dot(pw2[...], gh[y], NN) + dot(pw2[...], gl[y], NN) + synthesize_z(3, y)
        rows = pl.ds(y, 160, stride=16)
        cs[0, rows, :] = back[:, :128]
        cs[1, rows, :] = back[:, 128:]
        return 0

    lax.fori_loop(0, 16, last, 0)

    def write_grad(c, _):
        rows = pl.ds(c * 128, 128)
        v = jnp.concatenate([cs[0, rows, :], cs[1, rows, :]], axis=1)
        gf[c] = v.astype(BF16).reshape(8, 16, 256)
        return 0

    lax.fori_loop(0, C, write_grad, 0)

    for st in range(4):
        part = sy.at[st, :, pl.ds(0, 224), :]
        pltpu.make_async_copy(part, part, sy_sem.at[st]).wait()
        part = sx.at[st, pl.ds(0, 31 * 16)]
        pltpu.make_async_copy(part, part, sx_sem.at[st]).wait()
        part = sp.at[st, pl.ds(0, 31)]
        pltpu.make_async_copy(part, part, sp_sem.at[st]).wait()
    part = lr.at[pl.ds(0, 7)]
    pltpu.make_async_copy(part, part, l_sem.at[0]).wait()
    part = mr.at[pl.ds(0, 31)]
    pltpu.make_async_copy(part, part, l_sem.at[2]).wait()


def local(consts, field, cotangent, spectral_weight, pointwise_weight, bias):
    vmem = pl.BlockSpec(memory_space=pltpu.VMEM)
    dma = pltpu.SemaphoreType.DMA
    weights = jnp.transpose(spectral_weight, (1, 2, 3, 0, 4))
    scratch = [
        pltpu.VMEM((2, 2560, 128), F32),
        pltpu.VMEM((2, 2560, 128), F32),
        pltpu.VMEM((16, 160, 256), BF16),
        pltpu.VMEM((16, 160, 256), BF16),
        pltpu.VMEM((160, 160), BF16),
        pltpu.VMEM((160, 160), BF16),
        pltpu.VMEM((160, 128), F32),
        pltpu.VMEM((40, 128), F32),
        pltpu.VMEM((4, 4, 256, 128), F32),
        pltpu.VMEM((4, 4, 256, 128), F32),
        pltpu.VMEM((4, 512, 128), F32),
        pltpu.VMEM((4, 512, 128), F32),
        pltpu.VMEM((4, 32, 4, 128), F32),
        pltpu.VMEM((4, 32, 4, 128), F32),
        pltpu.VMEM((20, 120, 128), F32),
        pltpu.VMEM((128, 128), F32),
        pltpu.VMEM((480, 128), F32),
        pltpu.VMEM((480, 128), F32),
        pltpu.VMEM((120, 128), F32),
        pltpu.VMEM((120, 128), F32),
        pltpu.VMEM((480, 128), F32),
        pltpu.VMEM((480, 128), F32),
        pltpu.VMEM((176, 160), F32),
        pltpu.VMEM((32, 128), F32),
        pltpu.VMEM((8, 32, 128), F32),
        pltpu.VMEM((32, 128), F32),
        pltpu.VMEM((32, 32, 128), F32),
        dma((4,)), dma((4,)), dma((4,)), dma((4,)), dma((4,)), dma((4,)), dma((4,)),
    ]
    out, gf, gs, small = pl.pallas_call(
        kernel,
        out_shape=(
            jax.ShapeDtypeStruct((C, 8, 16, 256), BF16),
            jax.ShapeDtypeStruct((C, 8, 16, 256), BF16),
            jax.ShapeDtypeStruct((C, C, 3, 2, 72), F32),
            jax.ShapeDtypeStruct((32, 128), F32),
        ),
        in_specs=[vmem] * 14,
        out_specs=(vmem,) * 4,
        scratch_shapes=scratch,
        compiler_params=pltpu.CompilerParams(
            collective_id=0, has_side_effects=True, vmem_limit_bytes=58 << 20
        ),
        name="fourier_layer",
    )(field, cotangent, weights, pointwise_weight, bias.reshape(1, C), *consts)
    return (
        out,
        gf,
        jnp.transpose(gs, (3, 0, 1, 2, 4)),
        small[0:C, 0:C],
        small[C, 0:C],
    )


def solution(mesh):
    consts = [jnp.asarray(t) for t in tables()]
    placed = (
        P(None, "gx", "gy", None),
        P(None, "gx", "gy", None),
        P(None, None, None, "gy", "gx"),
        P(),
        P(),
    )
    return jax.shard_map(
        functools.partial(local, consts),
        mesh=mesh,
        in_specs=placed,
        out_specs=placed,
        check_vma=False,
    )
```

time: 811 us -> 148 us (0.18)
  waiting for transfers between devices: 386 us -> 0 us
  local copies, waits for them, and re-layouts: 188 us -> 7.88 us
  Pallas kernels: 0 us -> 140 us
  matrix products: 93.9 us -> 0 us
  blocking collectives: 91.2 us -> 0 us
  starting transfers between devices: 17.2 us -> 0 us
  between operations: 14.7 us -> 0.64 us
  other arithmetic: 12.6 us -> 0 us
    all_gather x4 -> x0, waiting for transfers between devices: 371 us -> none  [the longest x2 280 us: analyze(): portion = lax.all_gather(mode_data, 'gx', axis=3, tiled=True)]
    pallas_call x0 -> x1, Pallas kernels: none -> 140 us  [local(): pl.pallas_call(kernel, out_shape=(jax.ShapeDtypeStruct((C, 8, 16, 256), B...]
    dot_general x31 -> x0, matrix products: 93.9 us -> none  [the longest x2 15.1 us: synthesize(): jnp.einsum('km,zk->mz', flat, table_z, precision=PRECISE)]
    psum x1 -> x0, blocking collectives: 78.9 us -> none  [local(): lax.psum((local_weight, local_bias), ('gx', 'gy'))]
    unnamed x71 -> x7, local copies, waits for them, and re-layouts: 60.5 us -> 5.39 us
    squeeze x8 -> x1, local copies, waits for them, and re-layouts: 48.2 us -> 1.18 us  [local(): small[C, 0:C]]
    all_to_all x5 -> x0, local copies, waits for them, and re-layouts: 24.8 us -> none  [the longest x3 13.2 us: analyze(): lax.all_to_all(spectra, 'gy', split_axis=0, concat_axis=3, tiled=True)]
    slice x3 -> x1, local copies, waits for them, and re-layouts: 20.9 us -> 1.31 us  [local(): small[0:C, 0:C]]
  transfers between devices with their start and end apart: 7 -> 0, of which waited for: 5 -> 0; matrix products, arithmetic and copies ran while one was open for 4% -> 0% of each run, Pallas kernels for 0% -> 0%
where the time goes in v1:
time: 148 us
  Pallas kernels  140 us (95%)
  local copies, waits for them, and re-layouts  7.88 us (5%)
    pallas_call x1, Pallas kernels, local(): pl.pallas_call(kernel, out_shape=(jax.ShapeDtypeStruct((C, 8, 16, 256), B...  140 us
    unnamed x7, local copies, waits for them, and re-layouts  5.39 us

profile of v1, /device:TPU:1, one launch (start us, length us, event | category | flops | bytes accessed | tf_op | source)
XLA Modules:
  0.0 148.1 jit_solution(6108875209485009958)
XLA Ops:
  0.6 139.6 %fourier_layer.1 = (bf16[20,8,16,256]{3,2,1,0:T(8,128)(2,1)}, bf16[20,8,16,256]{3,2,1,0:T(8,128)(2,1)}, f32[20,20,3,2,72]{4,3,2,1,0:T(2,128)}, f32[32,128]{1,0:T(8,128)}) custom-call(bf16[20,8,16,256]{3,2,1,0:T(8,128)(2,1)} %field.1, bf16[20,8,16,256]{3,2,1,0:T(8,128)(2,1)} %cot.1, bf16[20,20,3,2,72]{4,3,2,1,0:T(2,128)(2,1)} %bitcast.6, bf16[20,20]{1,0:T(8,128)(2,1)} %pw.1, ...), custom_call_target="tpu_custom_call" | custom-call | tf_op jit(solution)/shard_map/fourier_layer/pallas_call | solution.py:535
  140.2 1.3 slice.6
  141.5 1.2 slice_bitcast_fusion
  142.7 0.0 copy-start
  142.7 2.6 %copy.22 = bf16[20,8,16,256]{3,2,1,0:T(8,128)(2,1)} copy(bf16[20,8,16,256]{3,2,1,0:T(8,128)(2,1)} %get-tuple-element.18) | data formatting | bytes 2621440
  145.3 0.0 copy-done
  145.3 0.0 copy-start.1
  145.3 1.1 copy.23
  146.4 0.7 copy-done.1
  147.1 1.0 copy.24
Async XLA Ops:
  142.7 2.6 %copy-start = (bf16[20,8,16,256]{3,2,1,0:T(8,128)(2,1)S(1)}, bf16[20,8,16,256]{3,2,1,0:T(8,128)(2,1)}, u32[]{:S(2)}) copy-start(bf16[20,8,16,256]{3,2,1,0:T(8,128)(2,1)} %get-tuple-element.19) | copy-start | bytes 3932164
  145.3 1.8 %copy-start.1 = (f32[20,20,3,2,72]{4,3,2,1,0:T(2,128)S(1)}, f32[20,20,3,2,72]{4,3,2,1,0:T(2,128)}, u32[]{:S(2)}) copy-start(f32[20,20,3,2,72]{4,3,2,1,0:T(2,128)} %get-tuple-element.11) | copy-start | bytes 2073604

commit v2 on v1

--- a/solution.py
+++ b/solution.py
@@ -66,6 +66,10 @@
     sel_o = np.asarray((sel_o & live).astype(BF16))
     sel_c = np.asarray((sel_c & live).astype(BF16))
     return tz, yh, yl, axh, axl, bxh, bxl, sel_o, sel_c
+
+
+def hops(k):
+    return min(k // 4, 8 - k // 4) + min(k % 4, 4 - k % 4)
 
 
 def iota(shape, axis):
@@ -134,9 +138,12 @@
             sy.at[st, :, own, :], ry.at[st, :, own, :], ry_sem.at[st]
         ).start()
 
+    gz, gw = g // 4, lax.rem(g, 4)
+    far_first = sorted(range(1, GX), key=hops, reverse=True)
+
     def send_gx(src, dst, ssem, rsem, size):
-        def body(k, _):
-            d = lax.rem(g + k, GX)
+        for k in far_first:
+            d = lax.rem(gz + k // 4, 8) * 4 + lax.rem(gw + k % 4, 4)
             pltpu.make_async_remote_copy(
                 src_ref=src.at[pl.ds(d * size, size)],
                 dst_ref=dst.at[pl.ds(g * size, size)],
@@ -145,9 +152,6 @@
                 device_id=(d, yy),
                 device_id_type=MESH,
             ).start()
-            return 0
-
-        lax.fori_loop(1, GX, body, 0)
         own = pl.ds(g * size, size)
         pltpu.make_async_copy(src.at[own], dst.at[own], rsem).start()
 
@@ -169,7 +173,7 @@
         fs[1, rows, :] = v[:, 128:]
         return 0
 
-    lax.fori_loop(0, C, widen, 0)
+    lax.fori_loop(0, C, widen, 0, unroll=4)
 
     def rows_of(ref, y):
         rows = pl.ds(y, 160, stride=16)
@@ -208,7 +212,7 @@
         analyze_z(0, y, s[0:48] + s[48:96])
         return 0
 
-    lax.fori_loop(0, 16, first_y, 0)
+    lax.fori_loop(0, 16, first_y, 0, unroll=4)
 
     pl.semaphore_wait(barrier, GY - 1 + GX - 1)
     send_y(0)
@@ -222,7 +226,7 @@
         return 0
 
     wf[...] = jnp.zeros_like(wf)
-    lax.fori_loop(0, C, widen_more, 0)
+    lax.fori_loop(0, C, widen_more, 0, unroll=4)
 
     pws[...] = jnp.zeros_like(pws)
     pws[0:20, 0:20] = pw[...].astype(F32)
@@ -363,7 +367,7 @@
         analyze_z(2, y, s)
         return 0
 
-    lax.fori_loop(0, 16, middle, 0)
+    lax.fori_loop(0, 16, middle, 0, unroll=4)
     send_y(2)
 
     row, col = iota((176, 160), 0), iota((176, 160), 1)
@@ -393,7 +397,7 @@
         out[c] = v.astype(BF16).reshape(8, 16, 256)
         return 0
 
-    lax.fori_loop(0, C, write_out, 0)
+    lax.fori_loop(0, C, write_out, 0, unroll=4)
 
     landed(ry.at[2], ry_sem.at[2])
     forward_y(2)
@@ -444,7 +448,7 @@
         q2[rows, :] = jnp.sum((wc * x2).reshape(5, 24, 128), axis=0)
         return 0
 
-    lax.fori_loop(0, C, unmix, 0)
+    lax.fori_loop(0, C, unmix, 0, unroll=2)
     modes(pick(sel_c[...], q1[...]), pick(sel_c[...], q2[...]), 3)
     send_p(3)
 
@@ -456,7 +460,7 @@
         gs[c] = v[:, 0:72].reshape(20, 3, 2, 72)
         return 0
 
-    lax.fori_loop(0, C, outer, 0)
+    lax.fori_loop(0, C, outer, 0, unroll=2)
 
     landed(rp.at[3], rp_sem.at[3])
     inverse_x(3)
@@ -475,7 +479,7 @@
         cs[1, rows, :] = back[:, 128:]
         return 0
 
-    lax.fori_loop(0, 16, last, 0)
+    lax.fori_loop(0, 16, last, 0, unroll=4)
 
     def write_grad(c, _):
         rows = pl.ds(c * 128, 128)
@@ -483,7 +487,7 @@
         gf[c] = v.astype(BF16).reshape(8, 16, 256)
         return 0
 
-    lax.fori_loop(0, C, write_grad, 0)
+    lax.fori_loop(0, C, write_grad, 0, unroll=4)
 
     for st in range(4):
         part = sy.at[st, :, pl.ds(0, 224), :]

time: 148 us -> 135 us (0.912)
  Pallas kernels: 140 us -> 126 us
    pallas_call x1, Pallas kernels: 140 us -> 126 us  [local(): pl.pallas_call(kernel, out_shape=(jax.ShapeDtypeStruct((C, 8, 16, 256), B...]
where the time goes in v2:
time: 135 us
  Pallas kernels  126 us (93%)
  local copies, waits for them, and re-layouts  7.88 us (6%)
    pallas_call x1, Pallas kernels, local(): pl.pallas_call(kernel, out_shape=(jax.ShapeDtypeStruct((C, 8, 16, 256), B...  126 us
    unnamed x7, local copies, waits for them, and re-layouts  5.39 us

profile of v2, /device:TPU:1, one launch (start us, length us, event | category | flops | bytes accessed | tf_op | source)
XLA Modules:
  0.0 134.8 jit_solution(3999898484445425860)
XLA Ops:
  0.6 126.2 %fourier_layer.1 = (bf16[20,8,16,256]{3,2,1,0:T(8,128)(2,1)}, bf16[20,8,16,256]{3,2,1,0:T(8,128)(2,1)}, f32[20,20,3,2,72]{4,3,2,1,0:T(2,128)}, f32[32,128]{1,0:T(8,128)}) custom-call(bf16[20,8,16,256]{3,2,1,0:T(8,128)(2,1)} %field.1, bf16[20,8,16,256]{3,2,1,0:T(8,128)(2,1)} %cot.1, bf16[20,20,3,2,72]{4,3,2,1,0:T(2,128)(2,1)} %bitcast.6, bf16[20,20]{1,0:T(8,128)(2,1)} %pw.1, ...), custom_call_target="tpu_custom_call" | custom-call | tf_op jit(solution)/shard_map/fourier_layer/pallas_call | solution.py:539
  126.9 1.3 slice.6
  128.2 1.2 slice_bitcast_fusion
  129.4 0.0 copy-start
  129.4 2.6 %copy.22 = bf16[20,8,16,256]{3,2,1,0:T(8,128)(2,1)} copy(bf16[20,8,16,256]{3,2,1,0:T(8,128)(2,1)} %get-tuple-element.18) | data formatting | bytes 2621440
  132.0 0.0 copy-done
  132.0 0.0 copy-start.1
  132.0 1.1 copy.23
  133.0 0.7 copy-done.1
  133.7 1.0 copy.24
Async XLA Ops:
  129.4 2.6 %copy-start = (bf16[20,8,16,256]{3,2,1,0:T(8,128)(2,1)S(1)}, bf16[20,8,16,256]{3,2,1,0:T(8,128)(2,1)}, u32[]{:S(2)}) copy-start(bf16[20,8,16,256]{3,2,1,0:T(8,128)(2,1)} %get-tuple-element.19) | copy-start | bytes 3932164
  132.0 1.8 %copy-start.1 = (f32[20,20,3,2,72]{4,3,2,1,0:T(2,128)S(1)}, f32[20,20,3,2,72]{4,3,2,1,0:T(2,128)}, u32[]{:S(2)}) copy-start(f32[20,20,3,2,72]{4,3,2,1,0:T(2,128)} %get-tuple-element.11) | copy-start | bytes 2073604

commit v3 on v2

--- a/solution.py
+++ b/solution.py
@@ -41,6 +41,7 @@
     y = np.zeros((8, 2, 16, 128))
     y[:, 0, :, 0:48], y[:, 0, :, 48:96] = cos, -sin
     y[:, 1, :, 0:48], y[:, 1, :, 48:96] = sin, cos
+    y = y.reshape(8, 2, 2, 8, 128).transpose(0, 2, 1, 3, 4)
     yh, yl = halves(y.reshape(256, 128))
 
     g = np.arange(GX)
@@ -98,8 +99,8 @@
     field, cot, w, pw, bias, tz, yh, yl, axh, axl, bxh, bxl, sel_o, sel_c,
     out, gf, gs, small,
     fs, cs, gh, gl, pw1, pw2, bb, pws, sy, ry, sx, rx, sp, rp, wf, tmp,
-    u1, u2, d1, d2, q1, q2, lw, ls, lr, ms, mr,
-    sy_sem, ry_sem, sx_sem, rx_sem, sp_sem, rp_sem, l_sem,
+    u1, u2, d1, d2, q1, q2, lw, ls, lr, ms, mr, out_v, gf_v, gs_v,
+    sy_sem, ry_sem, sx_sem, rx_sem, sp_sem, rp_sem, l_sem, o_sem,
 ):
     g = lax.axis_index("gx")
     yy = lax.axis_index("gy")
@@ -122,21 +123,28 @@
     lax.fori_loop(1, GY, greet_y, 0)
     lax.fori_loop(1, GX, greet_x, 0)
 
-    def send_y(st):
-        for k in range(1, GY):
-            d = lax.rem(yy + k, GY)
+    chip, core = yy // 2, lax.rem(yy, 2)
+    others_y = [
+        lax.rem(chip + n, 4) * 2 + (core if same else 1 - core)
+        for n, same in ((2, 1), (2, 0), (1, 1), (3, 1), (1, 0), (3, 0), (0, 0))
+    ]
+
+    def send_y(st, h):
+        sem_s, sem_r = sy_sem.at[2 * st + h], ry_sem.at[2 * st + h]
+        own = pl.ds(yy * 32 + h * 16, 16)
+        for d in others_y:
             pltpu.make_async_remote_copy(
-                src_ref=sy.at[st, :, pl.ds(d * 32, 32), :],
-                dst_ref=ry.at[st, :, pl.ds(yy * 32, 32), :],
-                send_sem=sy_sem.at[st],
-                recv_sem=ry_sem.at[st],
+                src_ref=sy.at[st, :, pl.ds(d * 32 + h * 16, 16), :],
+                dst_ref=ry.at[st, :, own, :],
+                send_sem=sem_s,
+                recv_sem=sem_r,
                 device_id=(g, d),
                 device_id_type=MESH,
             ).start()
-        own = pl.ds(yy * 32, 32)
-        pltpu.make_async_copy(
-            sy.at[st, :, own, :], ry.at[st, :, own, :], ry_sem.at[st]
-        ).start()
+        pltpu.make_async_copy(sy.at[st, :, own, :], ry.at[st, :, own, :], sem_r).start()
+
+    def landed_y(st, h):
+        landed(ry.at[st, :, pl.ds(0, 128), :], ry_sem.at[2 * st + h])
 
     gz, gw = g // 4, lax.rem(g, 4)
     far_first = sorted(range(1, GX), key=hops, reverse=True)
@@ -181,9 +189,9 @@
 
     pad_rows = jnp.zeros((96, 256), BF16)
 
-    def analyze_z(st, y, s):
+    def analyze_z(st, h, y, s):
         for r in range(2):
-            rows = pl.ds(r * 16 + y, 8, stride=32)
+            rows = pl.ds(h * 16 + r * 8 + y, 8, stride=32)
             tail = None
             for kz in range(3):
                 at = (kz * 2 + r) * 8
@@ -192,11 +200,11 @@
                 tail = piece if kz == 0 else tail + pltpu.roll(piece, 32 * kz, 1)
             sy[st, 3, rows, :] = tail
 
-    def synthesize_z(st, y):
+    def synthesize_z(st, h, y):
         main, tail = [], []
         for kz in range(3):
             for r in range(2):
-                rows = pl.ds(r * 16 + y, 8, stride=32)
+                rows = pl.ds(h * 16 + r * 8 + y, 8, stride=32)
                 main.append(ry[st, kz, rows, :])
                 piece = ry[st, 3, rows, :]
                 tail.append(piece if kz == 0 else pltpu.roll(piece, 128 - 32 * kz, 1))
@@ -206,16 +214,18 @@
         data = split(jnp.transpose(data)[:160])
         return dot3(data, (tz[0:48, :], tz[48:96, :]), NN)
 
-    def first_y(y, _):
-        f = jnp.concatenate([rows_of(fs, y).astype(BF16), pad_rows], axis=0)
+    def first_y(h, y, _):
+        f = jnp.concatenate([rows_of(fs, h * 8 + y).astype(BF16), pad_rows], axis=0)
         s = dot(tz[...], f, NT)
-        analyze_z(0, y, s[0:48] + s[48:96])
-        return 0
-
-    lax.fori_loop(0, 16, first_y, 0, unroll=4)
+        analyze_z(0, h, y, s[0:48] + s[48:96])
+        return 0
+
+    for h in range(2):
+        lax.fori_loop(0, 8, functools.partial(first_y, h), 0, unroll=4)
 
     pl.semaphore_wait(barrier, GY - 1 + GX - 1)
-    send_y(0)
+    send_y(0, 0)
+    send_y(0, 1)
 
     def widen_more(c, _):
         rows = pl.ds(c * 128, 128)
@@ -298,7 +308,8 @@
     zeroth = (row64 < 16) | ((row64 >= 48) & (row64 < 52))
     weight_z = jnp.where(zeroth & (yy == 0), 1.0 / CELLS, 2.0 / CELLS)
 
-    landed(ry.at[0], ry_sem.at[0])
+    landed_y(0, 0)
+    landed_y(0, 1)
     forward_y(0)
     send_x(0)
     landed(rx.at[0], rx_sem.at[0])
@@ -337,14 +348,15 @@
     send_x(1)
     landed(rx.at[1], rx_sem.at[1])
     inverse_y(1)
-    send_y(1)
-    landed(ry.at[1], ry_sem.at[1])
+    send_y(1, 0)
+    send_y(1, 1)
 
     lw[...] = jnp.zeros_like(lw)
     ones_rows = jnp.ones((16, 256), BF16)
 
-    def middle(y, _):
-        conv = synthesize_z(1, y)
+    def middle(h, y8, _):
+        conv = synthesize_z(1, h, y8)
+        y = h * 8 + y8
         f = rows_of(fs, y).astype(BF16)
         v = dot(pw1[...], f, NN) + jnp.concatenate([bb[...], bb[...]], axis=1) + conv
         square = v * v
@@ -364,11 +376,13 @@
         s = dot(tz[...], jnp.concatenate([high, pad_rows], axis=0), NT)
         s = s[0:48] + s[48:96]
         s = s + dot(tz[0:48, :], jnp.concatenate([low, pad_rows], axis=0), NT)
-        analyze_z(2, y, s)
-        return 0
-
-    lax.fori_loop(0, 16, middle, 0, unroll=4)
-    send_y(2)
+        analyze_z(2, h, y8, s)
+        return 0
+
+    for h in range(2):
+        landed_y(1, h)
+        lax.fori_loop(0, 8, functools.partial(middle, h), 0, unroll=4)
+        send_y(2, h)
 
     row, col = iota((176, 160), 0), iota((176, 160), 1)
     keep = (row >= 160) | (lax.rem(row, 8) == lax.rem(col, 8))
@@ -394,12 +408,14 @@
     def write_out(c, _):
         rows = pl.ds(c * 128, 128)
         v = jnp.concatenate([fs[0, rows, :], fs[1, rows, :]], axis=1)
-        out[c] = v.astype(BF16).reshape(8, 16, 256)
+        out_v[c] = v.astype(BF16).reshape(8, 16, 256)
         return 0
 
     lax.fori_loop(0, C, write_out, 0, unroll=4)
-
-    landed(ry.at[2], ry_sem.at[2])
+    pltpu.make_async_copy(out_v, out, o_sem.at[0]).start()
+
+    landed_y(2, 0)
+    landed_y(2, 1)
     forward_y(2)
     send_x(2)
 
@@ -457,10 +473,11 @@
         s1 = jnp.concatenate([u1[rows, :]] * 5, axis=0)
         s2 = jnp.concatenate([u2[rows, :]] * 5, axis=0)
         v = s1 * d1[...] + s2 * d2[...]
-        gs[c] = v[:, 0:72].reshape(20, 3, 2, 72)
+        gs_v[c] = v[:, 0:72].reshape(20, 3, 2, 72)
         return 0
 
     lax.fori_loop(0, C, outer, 0, unroll=2)
+    pltpu.make_async_copy(gs_v, gs, o_sem.at[1]).start()
 
     landed(rp.at[3], rp_sem.at[3])
     inverse_x(3)
@@ -469,29 +486,37 @@
     small[...] = jnp.sum(mr[...], axis=0) * (CELLS**-0.5)
     landed(rx.at[3], rx_sem.at[3])
     inverse_y(3)
-    send_y(3)
-    landed(ry.at[3], ry_sem.at[3])
-
-    def last(y, _):
-        back = dot(pw2[...], gh[y], NN) + dot(pw2[...], gl[y], NN) + synthesize_z(3, y)
+    send_y(3, 0)
+    send_y(3, 1)
+
+    def last(h, y8, _):
+        y = h * 8 + y8
+        back = dot(pw2[...], gh[y], NN) + dot(pw2[...], gl[y], NN)
+        back = back + synthesize_z(3, h, y8)
         rows = pl.ds(y, 160, stride=16)
         cs[0, rows, :] = back[:, :128]
         cs[1, rows, :] = back[:, 128:]
         return 0
 
-    lax.fori_loop(0, 16, last, 0, unroll=4)
+    for h in range(2):
+        landed_y(3, h)
+        lax.fori_loop(0, 8, functools.partial(last, h), 0, unroll=4)
 
     def write_grad(c, _):
         rows = pl.ds(c * 128, 128)
         v = jnp.concatenate([cs[0, rows, :], cs[1, rows, :]], axis=1)
-        gf[c] = v.astype(BF16).reshape(8, 16, 256)
-        return 0
-
-    lax.fori_loop(0, C, write_grad, 0, unroll=4)
+        gf_v[c] = v.astype(BF16).reshape(8, 16, 256)
+        return 0
+
+    for n in range(4):
+        lax.fori_loop(n * 5, n * 5 + 5, write_grad, 0, unroll=5)
+        part = pl.ds(n * 5, 5)
+        pltpu.make_async_copy(gf_v.at[part], gf.at[part], o_sem.at[2 + n]).start()
 
     for st in range(4):
-        part = sy.at[st, :, pl.ds(0, 224), :]
-        pltpu.make_async_copy(part, part, sy_sem.at[st]).wait()
+        part = sy.at[st, :, pl.ds(0, 112), :]
+        for h in range(2):
+            pltpu.make_async_copy(part, part, sy_sem.at[2 * st + h]).wait()
         part = sx.at[st, pl.ds(0, 31 * 16)]
         pltpu.make_async_copy(part, part, sx_sem.at[st]).wait()
         part = sp.at[st, pl.ds(0, 31)]
@@ -500,10 +525,37 @@
     pltpu.make_async_copy(part, part, l_sem.at[0]).wait()
     part = mr.at[pl.ds(0, 31)]
     pltpu.make_async_copy(part, part, l_sem.at[2]).wait()
+    pltpu.make_async_copy(out_v, out, o_sem.at[0]).wait()
+    pltpu.make_async_copy(gs_v, gs, o_sem.at[1]).wait()
+    for n in range(4):
+        part = pl.ds(n * 5, 5)
+        pltpu.make_async_copy(gf_v.at[part], gf.at[part], o_sem.at[2 + n]).wait()
+
+
+def deliver(out_a, gf_a, gs_a, small, out, gf, gs, gp, gb, out_v, gf_v, gs_v, sems):
+    there, back = [], []
+    for n in range(4):
+        part = pl.ds(n * 5, 5)
+        for i, (a, v, b) in enumerate(
+            ((out_a, out_v, out), (gf_a, gf_v, gf), (gs_a, gs_v, gs))
+        ):
+            sem = n * 3 + i
+            there.append(pltpu.make_async_copy(a.at[part], v.at[part], sems.at[sem]))
+            back.append(pltpu.make_async_copy(v.at[part], b.at[part], sems.at[12 + sem]))
+    for copy in there:
+        copy.start()
+    gp[...] = small[0:C, 0:C]
+    gb[...] = small[C : C + 1, 0:C]
+    for one, other in zip(there, back):
+        one.wait()
+        other.start()
+    for copy in back:
+        copy.wait()
 
 
 def local(consts, field, cotangent, spectral_weight, pointwise_weight, bias):
     vmem = pl.BlockSpec(memory_space=pltpu.VMEM)
+    anywhere = pl.BlockSpec(memory_space=pl.ANY)
     dma = pltpu.SemaphoreType.DMA
     weights = jnp.transpose(spectral_weight, (1, 2, 3, 0, 4))
     scratch = [
@@ -534,7 +586,10 @@
         pltpu.VMEM((8, 32, 128), F32),
         pltpu.VMEM((32, 128), F32),
         pltpu.VMEM((32, 32, 128), F32),
-        dma((4,)), dma((4,)), dma((4,)), dma((4,)), dma((4,)), dma((4,)), dma((4,)),
+        pltpu.VMEM((C, 8, 16, 256), BF16),
+        pltpu.VMEM((C, 8, 16, 256), BF16),
+        pltpu.VMEM((C, C, 3, 2, 72), F32),
+        dma((8,)), dma((8,)), dma((4,)), dma((4,)), dma((4,)), dma((4,)), dma((4,)), dma((6,)),
     ]
     out, gf, gs, small = pl.pallas_call(
         kernel,
@@ -545,20 +600,34 @@
             jax.ShapeDtypeStruct((32, 128), F32),
         ),
         in_specs=[vmem] * 14,
-        out_specs=(vmem,) * 4,
+        out_specs=(anywhere,) * 3 + (vmem,),
         scratch_shapes=scratch,
         compiler_params=pltpu.CompilerParams(
             collective_id=0, has_side_effects=True, vmem_limit_bytes=58 << 20
         ),
         name="fourier_layer",
     )(field, cotangent, weights, pointwise_weight, bias.reshape(1, C), *consts)
-    return (
-        out,
-        gf,
-        jnp.transpose(gs, (3, 0, 1, 2, 4)),
-        small[0:C, 0:C],
-        small[C, 0:C],
-    )
+    out, gf, gs, gp, gb = pl.pallas_call(
+        deliver,
+        out_shape=(
+            jax.ShapeDtypeStruct((C, 8, 16, 256), BF16),
+            jax.ShapeDtypeStruct((C, 8, 16, 256), BF16),
+            jax.ShapeDtypeStruct((C, C, 3, 2, 72), F32),
+            jax.ShapeDtypeStruct((C, C), F32),
+            jax.ShapeDtypeStruct((1, C), F32),
+        ),
+        in_specs=[anywhere] * 3 + [vmem],
+        out_specs=(anywhere,) * 3 + (vmem,) * 2,
+        scratch_shapes=[
+            pltpu.VMEM((C, 8, 16, 256), BF16),
+            pltpu.VMEM((C, 8, 16, 256), BF16),
+            pltpu.VMEM((C, C, 3, 2, 72), F32),
+            dma((24,)),
+        ],
+        compiler_params=pltpu.CompilerParams(vmem_limit_bytes=58 << 20),
+        name="deliver",
+    )(out, gf, gs, small)
+    return out, gf, jnp.transpose(gs, (3, 0, 1, 2, 4)), gp, gb.reshape(C)
 
 
 def solution(mesh):

time: 135 us -> 124 us (0.919)
  local copies, waits for them, and re-layouts: 7.88 us -> 0 us
  Pallas kernels: 126 us -> 124 us
    pallas_call x1, Pallas kernels: 126 us -> 119 us  [local(): pl.pallas_call(kernel, out_shape=(jax.ShapeDtypeStruct((C, 8, 16, 256), B...]
    unnamed x7 -> x0, local copies, waits for them, and re-layouts: 5.39 us -> none
    pallas_call x0 -> x1, Pallas kernels: none -> 4.71 us  [local(): pl.pallas_call(deliver, out_shape=(jax.ShapeDtypeStruct((C, 8, 16, 256),...]
where the time goes in v3:
time: 124 us
  Pallas kernels  124 us (100%)
    pallas_call x1, Pallas kernels, local(): pl.pallas_call(kernel, out_shape=(jax.ShapeDtypeStruct((C, 8, 16, 256), B...  119 us
    pallas_call x1, Pallas kernels, local(): pl.pallas_call(deliver, out_shape=(jax.ShapeDtypeStruct((C, 8, 16, 256),...  4.71 us

profile of v3, /device:TPU:1, one launch (start us, length us, event | category | flops | bytes accessed | tf_op | source)
XLA Modules:
  0.0 124.2 jit_solution(1225869182692627931)
XLA Ops:
  0.6 118.9 %fourier_layer.1 = (bf16[20,8,16,256]{3,2,1,0:T(8,128)(2,1)}, bf16[20,8,16,256]{3,2,1,0:T(8,128)(2,1)}, f32[20,20,3,2,72]{4,3,2,1,0:T(2,128)}, f32[32,128]{1,0:T(8,128)}) custom-call(bf16[20,8,16,256]{3,2,1,0:T(8,128)(2,1)} %field.1, bf16[20,8,16,256]{3,2,1,0:T(8,128)(2,1)} %cot.1, bf16[20,20,3,2,72]{4,3,2,1,0:T(2,128)(2,1)} %bitcast.4, bf16[20,20]{1,0:T(8,128)(2,1)} %pw.1, ...), custom_call_target="tpu_custom_call" | custom-call | tf_op jit(solution)/shard_map/fourier_layer/pallas_call | solution.py:594
  119.5 4.7 %deliver.1 = (bf16[20,8,16,256]{3,2,1,0:T(8,128)(2,1)}, bf16[20,8,16,256]{3,2,1,0:T(8,128)(2,1)}, f32[20,20,3,2,72]{4,3,2,1,0:T(2,128)}, f32[20,20]{1,0:T(8,128)}, f32[1,20]{1,0:T(1,128)}) custom-call(bf16[20,8,16,256]{3,2,1,0:T(8,128)(2,1)} %get-tuple-element.14.out_a, bf16[20,8,16,256]{3,2,1,0:T(8,128)(2,1)} %get-tuple-element.15.gf_a, ...), custom_call_target="tpu_custom_call" | custom-call | tf_op jit(solution)/shard_map/deliver/pallas_call | solution.py:610

commit v4 on v3

--- a/solution.py
+++ b/solution.py
@@ -143,31 +143,82 @@
             ).start()
         pltpu.make_async_copy(sy.at[st, :, own, :], ry.at[st, :, own, :], sem_r).start()
 
+    def send_y_tiles(st):
+        own = pl.ds(yy * 32 + 16, 16)
+        for t in range(4):
+            sem = 8 + st * 2 + t
+            for d in others_y:
+                pltpu.make_async_remote_copy(
+                    src_ref=sy.at[st, t, pl.ds(d * 32 + 16, 16), :],
+                    dst_ref=ry.at[st, t, own, :],
+                    send_sem=sy_sem.at[sem],
+                    recv_sem=ry_sem.at[sem],
+                    device_id=(g, d),
+                    device_id_type=MESH,
+                ).start()
+            pltpu.make_async_copy(
+                sy.at[st, t, own, :], ry.at[st, t, own, :], ry_sem.at[sem]
+            ).start()
+
     def landed_y(st, h):
         landed(ry.at[st, :, pl.ds(0, 128), :], ry_sem.at[2 * st + h])
 
     gz, gw = g // 4, lax.rem(g, 4)
     far_first = sorted(range(1, GX), key=hops, reverse=True)
 
-    def send_gx(src, dst, ssem, rsem, size):
+    def place(z, w):
+        return w * 8 + z
+
+    def send_gx(src, dst, ssem, rsem, size, to_owner):
+        mine = place(gz, gw)
+        to = g if to_owner else mine
         for k in far_first:
-            d = lax.rem(gz + k // 4, 8) * 4 + lax.rem(gw + k % 4, 4)
+            z, w = lax.rem(gz + k // 4, 8), lax.rem(gw + k % 4, 4)
+            at = place(z, w) if to_owner else z * 4 + w
             pltpu.make_async_remote_copy(
-                src_ref=src.at[pl.ds(d * size, size)],
-                dst_ref=dst.at[pl.ds(g * size, size)],
+                src_ref=src.at[pl.ds(at * size, size)],
+                dst_ref=dst.at[pl.ds(to * size, size)],
                 send_sem=ssem,
                 recv_sem=rsem,
-                device_id=(d, yy),
+                device_id=(z * 4 + w, yy),
                 device_id_type=MESH,
             ).start()
-        own = pl.ds(g * size, size)
-        pltpu.make_async_copy(src.at[own], dst.at[own], rsem).start()
+        own = mine if to_owner else g
+        pltpu.make_async_copy(
+            src.at[pl.ds(own * size, size)], dst.at[pl.ds(to * size, size)], rsem
+        ).start()
 
     def send_x(st):
-        send_gx(sx.at[st], rx.at[st], sx_sem.at[st], rx_sem.at[st], 16)
+        send_gx(sx.at[st], rx.at[st], sx_sem.at[st], rx_sem.at[st], 16, False)
 
     def send_p(st):
-        send_gx(sp.at[st], rp.at[st], sp_sem.at[st], rp_sem.at[st], 1)
+        send_gx(sp.at[st], rp.at[st], sp_sem.at[st], rp_sem.at[st], 1, st % 2 == 1)
+
+    def send_x_tile(st, t):
+        own = pl.ds(g * 16, 16)
+
+        def remote(z, at):
+            pltpu.make_async_remote_copy(
+                src_ref=sx.at[st, at],
+                dst_ref=rx.at[st, own],
+                send_sem=sx_sem.at[st],
+                recv_sem=rx_sem.at[st],
+                device_id=(z * 4 + t, yy),
+                device_id_type=MESH,
+            ).start()
+
+        for n in (4, 3, 5, 2, 6, 1, 7):
+            z = lax.rem(gz + n, 8)
+            remote(z, pl.ds(place(z, t) * 16, 16))
+        at = pl.ds(place(gz, t) * 16, 16)
+
+        @pl.when(gw != t)
+        def _():
+            remote(gz, at)
+
+        @pl.when(gw == t)
+        def _():
+            pltpu.make_async_copy(sx.at[st, at], rx.at[st, own], rx_sem.at[st]).start()
 
     def landed(ref, sem):
         pltpu.make_async_copy(ref, ref, sem).wait()
@@ -221,11 +272,11 @@
         return 0
 
     for h in range(2):
-        lax.fori_loop(0, 8, functools.partial(first_y, h), 0, unroll=4)
+        lax.fori_loop(0, 8, functools.partial(first_y, h), 0, unroll=8)
 
     pl.semaphore_wait(barrier, GY - 1 + GX - 1)
     send_y(0, 0)
-    send_y(0, 1)
+    send_y_tiles(0)
 
     def widen_more(c, _):
         rows = pl.ds(c * 128, 128)
@@ -254,9 +305,12 @@
     bb[...] = jnp.broadcast_to(column, (160, 128))
 
     def forward_y(st):
+        landed_y(st, 0)
         for t in range(4):
+            landed(ry.at[st, t, pl.ds(0, 128), :], ry_sem.at[8 + st * 2 + t])
             data = split(jnp.transpose(ry[st, t]))
             sx[st, pl.ds(t * 128, 128), :] = dot3(data, (yh[...], yl[...]), NN)
+            send_x_tile(st, t)
 
     def forward_x(st):
         p = dot3((axh[...], axl[...]), split(rx[st]), NN)
@@ -308,10 +362,7 @@
     zeroth = (row64 < 16) | ((row64 >= 48) & (row64 < 52))
     weight_z = jnp.where(zeroth & (yy == 0), 1.0 / CELLS, 2.0 / CELLS)
 
-    landed_y(0, 0)
-    landed_y(0, 1)
     forward_y(0)
-    send_x(0)
     landed(rx.at[0], rx_sem.at[0])
     forward_x(0)
     send_p(0)
@@ -340,7 +391,7 @@
         return a + wf[c] * sa, b + wf[c] * sb
 
     zero = jnp.zeros((120, 128), F32)
-    a, b = lax.fori_loop(0, C, mix, (zero, zero))
+    a, b = lax.fori_loop(0, C, mix, (zero, zero), unroll=4)
     modes(pick(sel_o[...], a) * weight_z, pick(sel_o[...], b) * weight_z, 1)
     send_p(1)
     landed(rp.at[1], rp_sem.at[1])
@@ -371,22 +422,25 @@
         high, low = split(grad)
         gh[y] = high
         gl[y] = low
-        f = jnp.concatenate([f, ones_rows], axis=0)
-        lw[...] += dot(f, high, NT) + dot(f, low, NT)
-        s = dot(tz[...], jnp.concatenate([high, pad_rows], axis=0), NT)
-        s = s[0:48] + s[48:96]
-        s = s + dot(tz[0:48, :], jnp.concatenate([low, pad_rows], axis=0), NT)
-        analyze_z(2, h, y8, s)
+        f = jnp.concatenate([tz[...], f, ones_rows], axis=0)
+        p = dot(f, jnp.concatenate([high, pad_rows], axis=0), NT)
+        f = jnp.concatenate([f[0:48], f[96:]], axis=0)
+        n = dot(f, jnp.concatenate([low, pad_rows], axis=0), NT)
+        lw[...] += p[96:] + n[48:]
+        analyze_z(2, h, y8, p[0:48] + p[48:96] + n[0:48])
         return 0
 
     for h in range(2):
         landed_y(1, h)
-        lax.fori_loop(0, 8, functools.partial(middle, h), 0, unroll=4)
-        send_y(2, h)
+        lax.fori_loop(0, 8, functools.partial(middle, h), 0, unroll=8)
+        if h == 0:
+            send_y(2, 0)
+        else:
+            send_y_tiles(2)
 
     row, col = iota((176, 160), 0), iota((176, 160), 1)
     keep = (row >= 160) | (lax.rem(row, 8) == lax.rem(col, 8))
-    total = jnp.where(keep, lw[...], 0.0)
+    total = jnp.where(keep, lw[:, 0:160], 0.0)
     row, col = iota((32, 176), 0), iota((32, 176), 1)
     left = ((col < 160) & (col // 8 == row)) | ((row == 20) & (col == 160))
     left = jnp.where(left, 1.0, 0.0).astype(BF16)
@@ -414,10 +468,7 @@
     lax.fori_loop(0, C, write_out, 0, unroll=4)
     pltpu.make_async_copy(out_v, out, o_sem.at[0]).start()
 
-    landed_y(2, 0)
-    landed_y(2, 1)
     forward_y(2)
-    send_x(2)
 
     landed(lr, l_sem.at[1])
     ms[...] = jnp.sum(lr[...], axis=0)
@@ -464,7 +515,7 @@
         q2[rows, :] = jnp.sum((wc * x2).reshape(5, 24, 128), axis=0)
         return 0
 
-    lax.fori_loop(0, C, unmix, 0, unroll=2)
+    lax.fori_loop(0, C, unmix, 0, unroll=4)
     modes(pick(sel_c[...], q1[...]), pick(sel_c[...], q2[...]), 3)
     send_p(3)
 
@@ -500,7 +551,7 @@
 
     for h in range(2):
         landed_y(3, h)
-        lax.fori_loop(0, 8, functools.partial(last, h), 0, unroll=4)
+        lax.fori_loop(0, 8, functools.partial(last, h), 0, unroll=8)
 
     def write_grad(c, _):
         rows = pl.ds(c * 128, 128)
@@ -515,8 +566,12 @@
 
     for st in range(4):
         part = sy.at[st, :, pl.ds(0, 112), :]
-        for h in range(2):
+        for h in range(2 if st % 2 == 1 else 1):
             pltpu.make_async_copy(part, part, sy_sem.at[2 * st + h]).wait()
+        if st % 2 == 0:
+            for t in range(4):
+                part = sy.at[st, t, pl.ds(0, 112), :]
+                pltpu.make_async_copy(part, part, sy_sem.at[8 + st * 2 + t]).wait()
         part = sx.at[st, pl.ds(0, 31 * 16)]
         pltpu.make_async_copy(part, part, sx_sem.at[st]).wait()
         part = sp.at[st, pl.ds(0, 31)]
@@ -581,7 +636,7 @@
         pltpu.VMEM((120, 128), F32),
         pltpu.VMEM((480, 128), F32),
         pltpu.VMEM((480, 128), F32),
-        pltpu.VMEM((176, 160), F32),
+        pltpu.VMEM((176, 256), F32),
         pltpu.VMEM((32, 128), F32),
         pltpu.VMEM((8, 32, 128), F32),
         pltpu.VMEM((32, 128), F32),
@@ -589,7 +644,7 @@
         pltpu.VMEM((C, 8, 16, 256), BF16),
         pltpu.VMEM((C, 8, 16, 256), BF16),
         pltpu.VMEM((C, C, 3, 2, 72), F32),
-        dma((8,)), dma((8,)), dma((4,)), dma((4,)), dma((4,)), dma((4,)), dma((4,)), dma((6,)),
+        dma((16,)), dma((16,)), dma((4,)), dma((4,)), dma((4,)), dma((4,)), dma((4,)), dma((6,)),
     ]
     out, gf, gs, small = pl.pallas_call(
         kernel,

time: 124 us -> 119 us (0.960)
  Pallas kernels: 124 us -> 118 us
    pallas_call x1, Pallas kernels: 119 us -> 114 us  [local(): pl.pallas_call(kernel, out_shape=(jax.ShapeDtypeStruct((C, 8, 16, 256), B...]
where the time goes in v4:
time: 119 us
  Pallas kernels  118 us (99%)
    pallas_call x1, Pallas kernels, local(): pl.pallas_call(kernel, out_shape=(jax.ShapeDtypeStruct((C, 8, 16, 256), B...  114 us
    pallas_call x1, Pallas kernels, local(): pl.pallas_call(deliver, out_shape=(jax.ShapeDtypeStruct((C, 8, 16, 256),...  4.71 us

profile of v4, /device:TPU:1, one launch (start us, length us, event | category | flops | bytes accessed | tf_op | source)
XLA Modules:
  0.0 119.2 jit_solution(7687129306033232040)
XLA Ops:
  0.6 113.7 %fourier_layer.1 = (bf16[20,8,16,256]{3,2,1,0:T(8,128)(2,1)}, bf16[20,8,16,256]{3,2,1,0:T(8,128)(2,1)}, f32[20,20,3,2,72]{4,3,2,1,0:T(2,128)}, f32[32,128]{1,0:T(8,128)}) custom-call(bf16[20,8,16,256]{3,2,1,0:T(8,128)(2,1)} %field.1, bf16[20,8,16,256]{3,2,1,0:T(8,128)(2,1)} %cot.1, bf16[20,20,3,2,72]{4,3,2,1,0:T(2,128)(2,1)} %bitcast.4, bf16[20,20]{1,0:T(8,128)(2,1)} %pw.1, ...), custom_call_target="tpu_custom_call" | custom-call | tf_op jit(solution)/shard_map/fourier_layer/pallas_call | solution.py:649
  114.3 4.7 %deliver.1 = (bf16[20,8,16,256]{3,2,1,0:T(8,128)(2,1)}, bf16[20,8,16,256]{3,2,1,0:T(8,128)(2,1)}, f32[20,20,3,2,72]{4,3,2,1,0:T(2,128)}, f32[20,20]{1,0:T(8,128)}, f32[1,20]{1,0:T(1,128)}) custom-call(bf16[20,8,16,256]{3,2,1,0:T(8,128)(2,1)} %get-tuple-element.14.out_a, bf16[20,8,16,256]{3,2,1,0:T(8,128)(2,1)} %get-tuple-element.15.gf_a, ...), custom_call_target="tpu_custom_call" | custom-call | tf_op jit(solution)/shard_map/deliver/pallas_call | solution.py:665

commit v5 on v4

--- a/solution.py
+++ b/solution.py
@@ -18,6 +18,7 @@
 MESH = pl.DeviceIdType.MESH
 NN = (((1,), (0,)), ((), ()))
 NT = (((1,), (1,)), ((), ()))
+TN = (((0,), (0,)), ((), ()))
 GELU_A = float(np.sqrt(2.0 / np.pi))
 GELU_B = 0.044715
 
@@ -99,7 +100,7 @@
     field, cot, w, pw, bias, tz, yh, yl, axh, axl, bxh, bxl, sel_o, sel_c,
     out, gf, gs, small,
     fs, cs, gh, gl, pw1, pw2, bb, pws, sy, ry, sx, rx, sp, rp, wf, tmp,
-    u1, u2, d1, d2, q1, q2, lw, ls, lr, ms, mr, out_v, gf_v, gs_v,
+    u1, u2, d1, d2, q1, q2, lw, ls, lr, ms, mr, out_v, gf_v, gs_v, pv, fb, tz3,
     sy_sem, ry_sem, sx_sem, rx_sem, sp_sem, rp_sem, l_sem, o_sem,
 ):
     g = lax.axis_index("gx")
@@ -262,8 +263,13 @@
         data = jnp.concatenate(
             [jnp.concatenate(main, axis=0), jnp.concatenate(tail, axis=0)], axis=1
         )
-        data = split(jnp.transpose(data)[:160])
-        return dot3(data, (tz[0:48, :], tz[48:96, :]), NN)
+        high, low = split(data)
+        data = jnp.concatenate([high, low, high], axis=0)
+        return dot(data[:, 0:160], tz3[...], TN)
+
+    tz3[0:48, :] = tz[0:48, :]
+    tz3[48:96, :] = tz[0:48, :]
+    tz3[96:144, :] = tz[48:96, :]
 
     def first_y(h, y, _):
         f = jnp.concatenate([rows_of(fs, h * 8 + y).astype(BF16), pad_rows], axis=0)
@@ -363,6 +369,14 @@
     weight_z = jnp.where(zeroth & (yy == 0), 1.0 / CELLS, 2.0 / CELLS)
 
     forward_y(0)
+
+    def ahead(y, _):
+        f = rows_of(fs, y).astype(BF16)
+        fb[y] = f
+        pv[y] = dot(pw1[...], f, NN) + jnp.concatenate([bb[...], bb[...]], axis=1)
+        return 0
+
+    lax.fori_loop(0, 16, ahead, 0, unroll=2)
     landed(rx.at[0], rx_sem.at[0])
     forward_x(0)
     send_p(0)
@@ -408,13 +422,13 @@
     def middle(h, y8, _):
         conv = synthesize_z(1, h, y8)
         y = h * 8 + y8
-        f = rows_of(fs, y).astype(BF16)
-        v = dot(pw1[...], f, NN) + jnp.concatenate([bb[...], bb[...]], axis=1) + conv
+        f = fb[y]
+        v = pv[y] + conv
         square = v * v
-        t = jnp.tanh(GELU_A * v * (1.0 + GELU_B * square))
-        half = 0.5 * (1.0 + t)
+        t = jnp.tanh(v * (GELU_A + (GELU_A * GELU_B) * square))
+        half = 0.5 + 0.5 * t
         act = v * half
-        slope = half + (0.5 * GELU_A) * v * (1.0 - t * t) * (1.0 + (3.0 * GELU_B) * square)
+        slope = half + act * (1.0 - half) * (2.0 * GELU_A + (6.0 * GELU_A * GELU_B) * square)
         grad = rows_of(cs, y) * slope
         rows = pl.ds(y, 160, stride=16)
         fs[0, rows, :] = act[:, :128]
@@ -533,6 +547,12 @@
     landed(rp.at[3], rp_sem.at[3])
     inverse_x(3)
     send_x(3)
+
+    def back_ahead(y, _):
+        pv[y] = dot(pw2[...], gh[y], NN) + dot(pw2[...], gl[y], NN)
+        return 0
+
+    lax.fori_loop(0, 16, back_ahead, 0, unroll=2)
     landed(mr, l_sem.at[3])
     small[...] = jnp.sum(mr[...], axis=0) * (CELLS**-0.5)
     landed(rx.at[3], rx_sem.at[3])
@@ -542,8 +562,7 @@
 
     def last(h, y8, _):
         y = h * 8 + y8
-        back = dot(pw2[...], gh[y], NN) + dot(pw2[...], gl[y], NN)
-        back = back + synthesize_z(3, h, y8)
+        back = pv[y] + synthesize_z(3, h, y8)
         rows = pl.ds(y, 160, stride=16)
         cs[0, rows, :] = back[:, :128]
         cs[1, rows, :] = back[:, 128:]
@@ -644,6 +663,9 @@
         pltpu.VMEM((C, 8, 16, 256), BF16),
         pltpu.VMEM((C, 8, 16, 256), BF16),
         pltpu.VMEM((C, C, 3, 2, 72), F32),
+        pltpu.VMEM((16, 160, 256), F32),
+        pltpu.VMEM((16, 160, 256), BF16),
+        pltpu.VMEM((144, 256), BF16),
         dma((16,)), dma((16,)), dma((4,)), dma((4,)), dma((4,)), dma((4,)), dma((4,)), dma((6,)),
     ]
     out, gf, gs, small = pl.pallas_call(

time: 119 us -> 117 us (0.983)
  Pallas kernels: 118 us -> 116 us
    pallas_call x1, Pallas kernels: 114 us -> 112 us  [local(): pl.pallas_call(kernel, out_shape=(jax.ShapeDtypeStruct((C, 8, 16, 256), B...]
where the time goes in v5:
time: 117 us
  Pallas kernels  116 us (99%)
    pallas_call x1, Pallas kernels, local(): pl.pallas_call(kernel, out_shape=(jax.ShapeDtypeStruct((C, 8, 16, 256), B...  112 us
    pallas_call x1, Pallas kernels, local(): pl.pallas_call(deliver, out_shape=(jax.ShapeDtypeStruct((C, 8, 16, 256),...  4.71 us

profile of v5, /device:TPU:1, one launch (start us, length us, event | category | flops | bytes accessed | tf_op | source)
XLA Modules:
  0.0 117.2 jit_solution(1725467781942323516)
XLA Ops:
  0.6 111.6 %fourier_layer.1 = (bf16[20,8,16,256]{3,2,1,0:T(8,128)(2,1)}, bf16[20,8,16,256]{3,2,1,0:T(8,128)(2,1)}, f32[20,20,3,2,72]{4,3,2,1,0:T(2,128)}, f32[32,128]{1,0:T(8,128)}) custom-call(bf16[20,8,16,256]{3,2,1,0:T(8,128)(2,1)} %field.1, bf16[20,8,16,256]{3,2,1,0:T(8,128)(2,1)} %cot.1, bf16[20,20,3,2,72]{4,3,2,1,0:T(2,128)(2,1)} %bitcast.4, bf16[20,20]{1,0:T(8,128)(2,1)} %pw.1, ...), custom_call_target="tpu_custom_call" | custom-call | tf_op jit(solution)/shard_map/fourier_layer/pallas_call | solution.py:671
  112.3 4.7 %deliver.1 = (bf16[20,8,16,256]{3,2,1,0:T(8,128)(2,1)}, bf16[20,8,16,256]{3,2,1,0:T(8,128)(2,1)}, f32[20,20,3,2,72]{4,3,2,1,0:T(2,128)}, f32[20,20]{1,0:T(8,128)}, f32[1,20]{1,0:T(1,128)}) custom-call(bf16[20,8,16,256]{3,2,1,0:T(8,128)(2,1)} %get-tuple-element.14.out_a, bf16[20,8,16,256]{3,2,1,0:T(8,128)(2,1)} %get-tuple-element.15.gf_a, ...), custom_call_target="tpu_custom_call" | custom-call | tf_op jit(solution)/shard_map/deliver/pallas_call | solution.py:687

commit v6 on v5

--- a/solution.py
+++ b/solution.py
@@ -460,7 +460,8 @@
     left = jnp.where(left, 1.0, 0.0).astype(BF16)
     high, low = split(pick(left, total))
     e128 = ones_e.astype(BF16)
-    ls[...] = dot(high, e128, NN) + dot(low, e128, NN)
+    packed = dot(high, e128, NN) + dot(low, e128, NN)
+    ls[...] = packed[0:8] + pltpu.roll(packed[8:16], 32, 1) + pltpu.roll(packed[16:24], 64, 1)
     for k in range(1, GY):
         d = lax.rem(yy + k, GY)
         pltpu.make_async_remote_copy(
@@ -473,6 +474,8 @@
         ).start()
     pltpu.make_async_copy(ls, lr.at[yy], l_sem.at[1]).start()
 
+    forward_y(2)
+
     def write_out(c, _):
         rows = pl.ds(c * 128, 128)
         v = jnp.concatenate([fs[0, rows, :], fs[1, rows, :]], axis=1)
@@ -481,26 +484,6 @@
 
     lax.fori_loop(0, C, write_out, 0, unroll=4)
     pltpu.make_async_copy(out_v, out, o_sem.at[0]).start()
-
-    forward_y(2)
-
-    landed(lr, l_sem.at[1])
-    ms[...] = jnp.sum(lr[...], axis=0)
-
-    def share(k, _):
-        d = lax.rem(g + k, GX)
-        pltpu.make_async_remote_copy(
-            src_ref=ms,
-            dst_ref=mr.at[g],
-            send_sem=l_sem.at[2],
-            recv_sem=l_sem.at[3],
-            device_id=(d, yy),
-            device_id_type=MESH,
-        ).start()
-        return 0
-
-    lax.fori_loop(1, GX, share, 0)
-    pltpu.make_async_copy(ms, mr.at[g], l_sem.at[3]).start()
 
     landed(rx.at[2], rx_sem.at[2])
     forward_x(2)
@@ -553,12 +536,29 @@
         return 0
 
     lax.fori_loop(0, 16, back_ahead, 0, unroll=2)
-    landed(mr, l_sem.at[3])
-    small[...] = jnp.sum(mr[...], axis=0) * (CELLS**-0.5)
     landed(rx.at[3], rx_sem.at[3])
     inverse_y(3)
     send_y(3, 0)
     send_y(3, 1)
+
+    landed(lr, l_sem.at[1])
+    ms[...] = jnp.sum(lr[...], axis=0)
+
+    def share(k, _):
+        d = lax.rem(g + k, GX)
+        pltpu.make_async_remote_copy(
+            src_ref=ms,
+            dst_ref=mr.at[g],
+            send_sem=l_sem.at[2],
+            recv_sem=l_sem.at[3],
+            device_id=(d, yy),
+            device_id_type=MESH,
+        ).start()
+        return 0
+
+    lax.fori_loop(1, GX, share, 0)
+    pltpu.make_async_copy(ms, mr.at[g], l_sem.at[3]).start()
+
 
     def last(h, y8, _):
         y = h * 8 + y8
@@ -577,6 +577,12 @@
         v = jnp.concatenate([cs[0, rows, :], cs[1, rows, :]], axis=1)
         gf_v[c] = v.astype(BF16).reshape(8, 16, 256)
         return 0
+
+    landed(mr, l_sem.at[3])
+    sums = jnp.sum(mr[...], axis=0) * (CELLS**-0.5)
+    small[0:8, :] = sums
+    small[8:16, :] = pltpu.roll(sums, 96, 1)
+    small[16:24, :] = pltpu.roll(sums, 64, 1)
 
     for n in range(4):
         lax.fori_loop(n * 5, n * 5 + 5, write_grad, 0, unroll=5)
@@ -656,10 +662,10 @@
         pltpu.VMEM((480, 128), F32),
         pltpu.VMEM((480, 128), F32),
         pltpu.VMEM((176, 256), F32),
-        pltpu.VMEM((32, 128), F32),
-        pltpu.VMEM((8, 32, 128), F32),
-        pltpu.VMEM((32, 128), F32),
-        pltpu.VMEM((32, 32, 128), F32),
+        pltpu.VMEM((8, 128), F32),
+        pltpu.VMEM((8, 8, 128), F32),
+        pltpu.VMEM((8, 128), F32),
+        pltpu.VMEM((32, 8, 128), F32),
         pltpu.VMEM((C, 8, 16, 256), BF16),
         pltpu.VMEM((C, 8, 16, 256), BF16),
         pltpu.VMEM((C, C, 3, 2, 72), F32),
@@ -674,7 +680,7 @@
             jax.ShapeDtypeStruct((C, 8, 16, 256), BF16),
             jax.ShapeDtypeStruct((C, 8, 16, 256), BF16),
             jax.ShapeDtypeStruct((C, C, 3, 2, 72), F32),
-            jax.ShapeDtypeStruct((32, 128), F32),
+            jax.ShapeDtypeStruct((24, 128), F32),
         ),
         in_specs=[vmem] * 14,
         out_specs=(anywhere,) * 3 + (vmem,),

time: 117 us -> 110 us (0.940)
  Pallas kernels: 116 us -> 110 us
    pallas_call x1, Pallas kernels: 112 us -> 105 us  [local(): pl.pallas_call(kernel, out_shape=(jax.ShapeDtypeStruct((C, 8, 16, 256), B...]
where the time goes in v6:
time: 110 us
  Pallas kernels  110 us (100%)
    pallas_call x1, Pallas kernels, local(): pl.pallas_call(kernel, out_shape=(jax.ShapeDtypeStruct((C, 8, 16, 256), B...  105 us
    pallas_call x1, Pallas kernels, local(): pl.pallas_call(deliver, out_shape=(jax.ShapeDtypeStruct((C, 8, 16, 256),...  4.7 us

profile of v6, /device:TPU:1, one launch (start us, length us, event | category | flops | bytes accessed | tf_op | source)
XLA Modules:
  0.0 110.3 jit_solution(901347119180027865)
XLA Ops:
  0.6 104.8 %fourier_layer.1 = (bf16[20,8,16,256]{3,2,1,0:T(8,128)(2,1)}, bf16[20,8,16,256]{3,2,1,0:T(8,128)(2,1)}, f32[20,20,3,2,72]{4,3,2,1,0:T(2,128)}, f32[24,128]{1,0:T(8,128)}) custom-call(bf16[20,8,16,256]{3,2,1,0:T(8,128)(2,1)} %field.1, bf16[20,8,16,256]{3,2,1,0:T(8,128)(2,1)} %cot.1, bf16[20,20,3,2,72]{4,3,2,1,0:T(2,128)(2,1)} %bitcast.4, bf16[20,20]{1,0:T(8,128)(2,1)} %pw.1, ...), custom_call_target="tpu_custom_call" | custom-call | tf_op jit(solution)/shard_map/fourier_layer/pallas_call | solution.py:677
  105.5 4.7 %deliver.1 = (bf16[20,8,16,256]{3,2,1,0:T(8,128)(2,1)}, bf16[20,8,16,256]{3,2,1,0:T(8,128)(2,1)}, f32[20,20,3,2,72]{4,3,2,1,0:T(2,128)}, f32[20,20]{1,0:T(8,128)}, f32[1,20]{1,0:T(1,128)}) custom-call(bf16[20,8,16,256]{3,2,1,0:T(8,128)(2,1)} %get-tuple-element.14.out_a, bf16[20,8,16,256]{3,2,1,0:T(8,128)(2,1)} %get-tuple-element.15.gf_a, ...), custom_call_target="tpu_custom_call" | custom-call | tf_op jit(solution)/shard_map/deliver/pallas_call | solution.py:693

commit v7 on v6

--- a/solution.py
+++ b/solution.py
@@ -267,9 +267,6 @@
         data = jnp.concatenate([high, low, high], axis=0)
         return dot(data[:, 0:160], tz3[...], TN)
 
-    tz3[0:48, :] = tz[0:48, :]
-    tz3[48:96, :] = tz[0:48, :]
-    tz3[96:144, :] = tz[48:96, :]
 
     def first_y(h, y, _):
         f = jnp.concatenate([rows_of(fs, h * 8 + y).astype(BF16), pad_rows], axis=0)
@@ -284,16 +281,65 @@
     send_y(0, 0)
     send_y_tiles(0)
 
-    def widen_more(c, _):
-        rows = pl.ds(c * 128, 128)
-        v = cot[c].astype(F32).reshape(128, 256)
-        cs[0, rows, :] = v[:, :128]
-        cs[1, rows, :] = v[:, 128:]
-        wf[c, :, 0:72] = w[c].astype(F32).reshape(120, 72)
-        return 0
-
-    wf[...] = jnp.zeros_like(wf)
-    lax.fori_loop(0, C, widen_more, 0, unroll=4)
+    def forward_y(st):
+        landed_y(st, 0)
+        for t in range(4):
+            landed(ry.at[st, t, pl.ds(0, 128), :], ry_sem.at[8 + st * 2 + t])
+            data = split(jnp.transpose(ry[st, t]))
+            sx[st, pl.ds(t * 128, 128), :] = dot3(data, (yh[...], yl[...]), NN)
+            send_x_tile(st, t)
+
+    def forward_x(st):
+        p = dot3((axh[...], axl[...]), split(rx[st]), NN)
+        pc, ps = p[:128], p[128:]
+        side = iota((128, 128), 1) < 48
+        o = pc + jnp.where(side, pltpu.roll(ps, 80, 1), -pltpu.roll(ps, 48, 1))
+        sp[st] = o.reshape(32, 4, 128)
+
+    def spectrum(st):
+        tmp[...] = rp[st].reshape(128, 128)
+        k0 = tmp[pl.ds(0, 64, stride=2), :]
+        k1 = tmp[pl.ds(1, 64, stride=2), :]
+        roll = lambda v, n: pltpu.roll(v, n, 1)
+        re_e = jnp.where(lane < 48, k0, roll(k1, 48))
+        im_e = jnp.where(lane < 48, roll(k0, 80), k1)
+        re_o = jnp.where(lane < 24, roll(k0, 104), roll(k1, 24))
+        im_o = jnp.where(lane < 24, roll(k0, 56), roll(k1, 104))
+        live = lane < 72
+        re = jnp.where(live, jnp.where(even, re_e, re_o), 0.0)
+        im = jnp.where(live, jnp.where(even, im_e, im_o), 0.0)
+        return re, im
+
+    def modes(re, im, st):
+        roll = lambda v, n: pltpu.roll(v, n, 1)
+        within = lambda a, b: (lane >= a) & (lane < b)
+        zero = jnp.zeros((64, 128), F32)
+        e0 = jnp.where(lane < 48, re, jnp.where(within(48, 96), roll(im, 48), zero))
+        e1 = jnp.where(lane < 24, roll(re, 80), jnp.where(within(48, 72), im, zero))
+        o0 = jnp.where(
+            within(24, 48), roll(re, 24), jnp.where(within(72, 96), roll(im, 72), zero)
+        )
+        o1 = jnp.where(lane < 48, roll(re, 104), jnp.where(within(48, 96), roll(im, 24), zero))
+        tmp[pl.ds(0, 64, stride=2), :] = jnp.where(even, e0, o0)
+        tmp[pl.ds(1, 64, stride=2), :] = jnp.where(even, e1, o1)
+        sp[st] = tmp[...].reshape(32, 4, 128)
+
+    def inverse_x(st):
+        p = dot3((bxh[...], bxl[...]), split(rp[st].reshape(128, 128)), NN)
+        pc, ps = p[:512], p[512:]
+        side = iota((512, 128), 1) < 48
+        sx[st] = pc + jnp.where(side, -pltpu.roll(ps, 80, 1), pltpu.roll(ps, 48, 1))
+
+    def inverse_y(st):
+        for t in range(4):
+            data = split(rx[st, pl.ds(t * 128, 128), :])
+            sy[st, t] = dot3((yh[...], yl[...]), data, NT)
+
+    row64 = iota((64, 128), 0)
+    zeroth = (row64 < 16) | ((row64 >= 48) & (row64 < 52))
+    weight_z = jnp.where(zeroth & (yy == 0), 1.0 / CELLS, 2.0 / CELLS)
+
+    forward_y(0)
 
     pws[...] = jnp.zeros_like(pws)
     pws[0:20, 0:20] = pw[...].astype(F32)
@@ -309,77 +355,16 @@
     pw2[...] = jnp.where(same_x, dot(t, e, NT), 0.0).astype(BF16)
     column = jnp.sum(ones_e * pws[32:33, :], axis=1, keepdims=True)
     bb[...] = jnp.broadcast_to(column, (160, 128))
-
-    def forward_y(st):
-        landed_y(st, 0)
-        for t in range(4):
-            landed(ry.at[st, t, pl.ds(0, 128), :], ry_sem.at[8 + st * 2 + t])
-            data = split(jnp.transpose(ry[st, t]))
-            sx[st, pl.ds(t * 128, 128), :] = dot3(data, (yh[...], yl[...]), NN)
-            send_x_tile(st, t)
-
-    def forward_x(st):
-        p = dot3((axh[...], axl[...]), split(rx[st]), NN)
-        pc, ps = p[:128], p[128:]
-        side = iota((128, 128), 1) < 48
-        o = pc + jnp.where(side, pltpu.roll(ps, 80, 1), -pltpu.roll(ps, 48, 1))
-        sp[st] = o.reshape(32, 4, 128)
-
-    def spectrum(st):
-        tmp[...] = rp[st].reshape(128, 128)
-        k0 = tmp[pl.ds(0, 64, stride=2), :]
-        k1 = tmp[pl.ds(1, 64, stride=2), :]
-        roll = lambda v, n: pltpu.roll(v, n, 1)
-        re_e = jnp.where(lane < 48, k0, roll(k1, 48))
-        im_e = jnp.where(lane < 48, roll(k0, 80), k1)
-        re_o = jnp.where(lane < 24, roll(k0, 104), roll(k1, 24))
-        im_o = jnp.where(lane < 24, roll(k0, 56), roll(k1, 104))
-        live = lane < 72
-        re = jnp.where(live, jnp.where(even, re_e, re_o), 0.0)
-        im = jnp.where(live, jnp.where(even, im_e, im_o), 0.0)
-        return re, im
-
-    def modes(re, im, st):
-        roll = lambda v, n: pltpu.roll(v, n, 1)
-        within = lambda a, b: (lane >= a) & (lane < b)
-        zero = jnp.zeros((64, 128), F32)
-        e0 = jnp.where(lane < 48, re, jnp.where(within(48, 96), roll(im, 48), zero))
-        e1 = jnp.where(lane < 24, roll(re, 80), jnp.where(within(48, 72), im, zero))
-        o0 = jnp.where(
-            within(24, 48), roll(re, 24), jnp.where(within(72, 96), roll(im, 72), zero)
-        )
-        o1 = jnp.where(lane < 48, roll(re, 104), jnp.where(within(48, 96), roll(im, 24), zero))
-        tmp[pl.ds(0, 64, stride=2), :] = jnp.where(even, e0, o0)
-        tmp[pl.ds(1, 64, stride=2), :] = jnp.where(even, e1, o1)
-        sp[st] = tmp[...].reshape(32, 4, 128)
-
-    def inverse_x(st):
-        p = dot3((bxh[...], bxl[...]), split(rp[st].reshape(128, 128)), NN)
-        pc, ps = p[:512], p[512:]
-        side = iota((512, 128), 1) < 48
-        sx[st] = pc + jnp.where(side, -pltpu.roll(ps, 80, 1), pltpu.roll(ps, 48, 1))
-
-    def inverse_y(st):
-        for t in range(4):
-            data = split(rx[st, pl.ds(t * 128, 128), :])
-            sy[st, t] = dot3((yh[...], yl[...]), data, NT)
-
-    row64 = iota((64, 128), 0)
-    zeroth = (row64 < 16) | ((row64 >= 48) & (row64 < 52))
-    weight_z = jnp.where(zeroth & (yy == 0), 1.0 / CELLS, 2.0 / CELLS)
-
-    forward_y(0)
-
-    def ahead(y, _):
-        f = rows_of(fs, y).astype(BF16)
-        fb[y] = f
-        pv[y] = dot(pw1[...], f, NN) + jnp.concatenate([bb[...], bb[...]], axis=1)
-        return 0
-
-    lax.fori_loop(0, 16, ahead, 0, unroll=2)
     landed(rx.at[0], rx_sem.at[0])
     forward_x(0)
     send_p(0)
+
+    def widen_weights(c, _):
+        wf[c, :, 0:72] = w[c].astype(F32).reshape(120, 72)
+        return 0
+
+    wf[...] = jnp.zeros_like(wf)
+    lax.fori_loop(0, C, widen_weights, 0, unroll=4)
     landed(rp.at[0], rp_sem.at[0])
     re, im = spectrum(0)
     for kz in range(3):
@@ -408,9 +393,30 @@
     a, b = lax.fori_loop(0, C, mix, (zero, zero), unroll=4)
     modes(pick(sel_o[...], a) * weight_z, pick(sel_o[...], b) * weight_z, 1)
     send_p(1)
+
+    tz3[0:48, :] = tz[0:48, :]
+    tz3[48:96, :] = tz[0:48, :]
+    tz3[96:144, :] = tz[48:96, :]
+
+    def widen_cotangent(c, _):
+        rows = pl.ds(c * 128, 128)
+        v = cot[c].astype(F32).reshape(128, 256)
+        cs[0, rows, :] = v[:, :128]
+        cs[1, rows, :] = v[:, 128:]
+        return 0
+
+    lax.fori_loop(0, C, widen_cotangent, 0, unroll=4)
     landed(rp.at[1], rp_sem.at[1])
     inverse_x(1)
     send_x(1)
+
+    def ahead(y, _):
+        f = rows_of(fs, y).astype(BF16)
+        fb[y] = f
+        pv[y] = dot(pw1[...], f, NN) + jnp.concatenate([bb[...], bb[...]], axis=1)
+        return 0
+
+    lax.fori_loop(0, 16, ahead, 0, unroll=2)
     landed(rx.at[1], rx_sem.at[1])
     inverse_y(1)
     send_y(1, 0)

time: 110 us -> 110 us (level)
  no operation moved by 1% of the time
where the time goes in v7:
time: 110 us
  Pallas kernels  109 us (99%)
    pallas_call x1, Pallas kernels, local(): pl.pallas_call(kernel, out_shape=(jax.ShapeDtypeStruct((C, 8, 16, 256), B...  104 us
    pallas_call x1, Pallas kernels, local(): pl.pallas_call(deliver, out_shape=(jax.ShapeDtypeStruct((C, 8, 16, 256),...  4.7 us

profile of v7, /device:TPU:1, one launch (start us, length us, event | category | flops | bytes accessed | tf_op | source)
XLA Modules:
  0.0 109.8 jit_solution(4819377945272366298)
XLA Ops:
  0.6 104.3 %fourier_layer.1 = (bf16[20,8,16,256]{3,2,1,0:T(8,128)(2,1)}, bf16[20,8,16,256]{3,2,1,0:T(8,128)(2,1)}, f32[20,20,3,2,72]{4,3,2,1,0:T(2,128)}, f32[24,128]{1,0:T(8,128)}) custom-call(bf16[20,8,16,256]{3,2,1,0:T(8,128)(2,1)} %field.1, bf16[20,8,16,256]{3,2,1,0:T(8,128)(2,1)} %cot.1, bf16[20,20,3,2,72]{4,3,2,1,0:T(2,128)(2,1)} %bitcast.4, bf16[20,20]{1,0:T(8,128)(2,1)} %pw.1, ...), custom_call_target="tpu_custom_call" | custom-call | tf_op jit(solution)/shard_map/fourier_layer/pallas_call | solution.py:683
  104.9 4.7 %deliver.1 = (bf16[20,8,16,256]{3,2,1,0:T(8,128)(2,1)}, bf16[20,8,16,256]{3,2,1,0:T(8,128)(2,1)}, f32[20,20,3,2,72]{4,3,2,1,0:T(2,128)}, f32[20,20]{1,0:T(8,128)}, f32[1,20]{1,0:T(1,128)}) custom-call(bf16[20,8,16,256]{3,2,1,0:T(8,128)(2,1)} %get-tuple-element.14.out_a, bf16[20,8,16,256]{3,2,1,0:T(8,128)(2,1)} %get-tuple-element.15.gf_a, ...), custom_call_target="tpu_custom_call" | custom-call | tf_op jit(solution)/shard_map/deliver/pallas_call | solution.py:699
